TPU v7x, 32 devices: a whole 2x2x4 slice. The times are simulated.
32 devices in a mesh: dp: 8 (over z, y), tensor: 4 (over x, core).
Axes of the slice: x: 2, y: 2, z: 4, core: 2. Of those that a mesh axis runs over, the one named last changes fastest.
Arguments:
- tokens: bfloat16 [8192, 1536], P('dp'), may hold values from -6 to 6
- segment: int32 [8192], P('dp'), may hold values from -1 to 7, as said below
- norm_gain: float32 [1536], replicated, may hold values from 0.5 to 1.5
- gate_weight: bfloat16 [1536, 3072], P(None, 'tensor'), may hold values from -0.15625 to 0.15625
- value_weight: bfloat16 [1536, 3072], P(None, 'tensor'), may hold values from -0.15625 to 0.15625
- state_weight: bfloat16 [1536, 256], replicated, may hold values from -0.15625 to 0.15625
- step_weight: bfloat16 [1536, 48], P(None, 'tensor'), may hold values from -0.15625 to 0.15625
- value_filter: float32 [4, 3072], P(None, 'tensor'), may hold values from -3 to 3
- value_offset: float32 [3072], P('tensor'), may hold values from -3 to 3
- state_filter: float32 [4, 256], replicated, may hold values from -3 to 3
- state_offset: float32 [256], replicated, may hold values from -3 to 3
- step_offset: float32 [48], P('tensor'), may hold values from -6.9 to -2.3
- decay_log: float32 [48], P('tensor'), may hold values from 0 to 2.77
- skip_gain: float32 [48], P('tensor'), may hold values from 0.5 to 1.5
- inner_gain: float32 [3072], P('tensor'), may hold values from 0.1 to 1.9
- output_weight: bfloat16 [3072, 1536], P('tensor'), may hold values from -0.109375 to 0.109375
- cotangent: bfloat16 [8192, 1536], P('dp'), may hold values from -6 to 6
Outputs:
- mixed: bfloat16 [8192, 1536], P('dp', 'tensor')
- tokens_grad: float32 [8192, 1536], P('dp', 'tensor')
- norm_gain_grad: float32 [1536], replicated
- gate_weight_grad: float32 [1536, 3072], P(None, 'tensor')
- value_weight_grad: float32 [1536, 3072], P(None, 'tensor')
- state_weight_grad: float32 [1536, 256], replicated
- step_weight_grad: float32 [1536, 48], P(None, 'tensor')
- value_filter_grad: float32 [4, 3072], P(None, 'tensor')
- value_offset_grad: float32 [3072], P('tensor')
- state_filter_grad: float32 [4, 256], replicated
- state_offset_grad: float32 [256], replicated
- step_offset_grad: float32 [48], P('tensor')
- decay_log_grad: float32 [48], P('tensor')
- skip_gain_grad: float32 [48], P('tensor')
- inner_gain_grad: float32 [3072], P('tensor')
- output_weight_grad: float32 [3072, 1536], P('tensor')
Inputs may be any that keep to these rules, and one draw needn't show every extreme that they name: `segment`: within one device's 1024 slots the live tokens come first and the empty slots (id -1) last; a sequence is a run of equal ids among live tokens, ids counting up from 0 along the slots; each has 128 to 1024 tokens except that a device's last live one may be shorter; some device's first sequence has exactly 1024 tokens; each device holds 512 to 1024 live tokens, some device exactly 1024; some device reaches the largest id.
All inputs are finite; a program needn't handle non-finite values.
Results may differ from a plain program's by a relative error of at most 0.0081.
Values sent between devices are 32-bit elements; how exact they have to be, the bound alone decides.
No kernel may reach another device: no remote copies, remote signals or barrier semaphores. Data moves between devices by JAX's collectives and lax.ppermute only.
A program may use at most 192 MiB of HBM per device.

v0:
```python
import jax
import jax.numpy as jnp
from jax import lax
from jax.experimental import pallas as pl
from jax.experimental.pallas import tpu as pltpu
from jax.sharding import PartitionSpec as P


CONV = 4
CHUNK = 128
EPS = 1e-05
HIGH = lax.Precision.HIGHEST
F32 = jnp.float32
BF16 = jnp.bfloat16
FAR = -1e30


def nn(a, b, precision=None):
    return lax.dot_general(
        a, b, (((1,), (0,)), ((), ())), precision=precision, preferred_element_type=F32
    )


def nt(a, b, precision=None):
    return lax.dot_general(
        a, b, (((1,), (1,)), ((), ())), precision=precision, preferred_element_type=F32
    )


def tn(a, b, precision=None):
    return lax.dot_general(
        a, b, (((0,), (0,)), ((), ())), precision=precision, preferred_element_type=F32
    )


def halves(a):
    upper = a.astype(BF16)
    return upper, (a - upper.astype(F32)).astype(BF16)


def sigmoid(v):
    return 0.5 * jnp.tanh(0.5 * v) + 0.5


def softplus(v):
    return jnp.maximum(v, 0.0) + jnp.log1p(jnp.exp(-jnp.abs(v)))


def head_map(heads, channels):
    width = channels // heads
    owner = lax.broadcasted_iota(jnp.int32, (heads, channels), 1) // width
    mine = lax.broadcasted_iota(jnp.int32, (heads, channels), 0)
    return (owner == mine).astype(BF16)


def spread(columns, head_of):
    upper, lower = halves(columns)
    both = jnp.concatenate([upper.astype(F32), lower.astype(F32)], axis=1).astype(BF16)
    return nn(both, jnp.concatenate([head_of, head_of], axis=0))


def gather(wide, head_of):
    upper, lower = halves(wide)
    return nt(upper, head_of) + nt(lower, head_of)


def convolve(ext, signal, before, aux, weights, offset):
    rows = signal.shape[0]
    ext[0:8, :] = before
    ext[8 : 8 + rows, :] = signal
    total = offset + weights[0:1, :] * signal
    for back in range(1, CONV):
        moved = ext[8 - back : 8 - back + rows, :]
        total = total + weights[back : back + 1, :] * (moved * aux[:, back - 1 : back])
    return total


def unfilter(ext, later, sums, grad, signal, aux, weights):
    rows = signal.shape[0]
    ext[0:rows, :] = grad
    ext[rows : rows + 8, :] = later[...]
    later[...] = grad[0:8, :]
    total = weights[0:1, :] * grad
    sums[0:1, :] += jnp.sum(grad * signal, axis=0, keepdims=True)
    for back in range(1, CONV):
        ahead = ext[back : back + rows, :] * aux[:, 2 + back : 3 + back]
        total = total + weights[back : back + 1, :] * ahead
        sums[back : back + 1, :] += jnp.sum(ahead * signal, axis=0, keepdims=True)
    sums[4:5, :] += jnp.sum(grad, axis=0, keepdims=True)
    return total


def triangle(rows):
    down = lax.broadcasted_iota(jnp.int32, (rows, rows), 0)
    along = lax.broadcasted_iota(jnp.int32, (rows, rows), 1)
    return down >= along


def decays(raw, offset, decay, tri):
    moved = raw + offset
    steps = softplus(moved)
    rates = steps * (-jnp.exp(decay))
    total = nn(tri, rates, HIGH)
    total_rows = lax.dot_general(
        rates, tri, (((0,), (1,)), ((), ())), precision=HIGH, preferred_element_type=F32
    )
    return moved, steps, rates, total, total_rows


def forward_kernel(
    ends,
    aux_ref,
    seg_ref,
    u_ref,
    s_ref,
    raw_ref,
    gate_ref,
    bg_ref,
    vf_ref,
    vo_ref,
    sf_ref,
    so_ref,
    off_ref,
    dec_ref,
    skip_ref,
    ig_ref,
    y_ref,
    sum_ref,
    kept_ref,
    uext,
    sext,
    uold,
    sold,
    state,
):
    i = pl.program_id(0)
    rows, channels = u_ref.shape
    heads = raw_ref.shape[1]
    half = s_ref.shape[1] // 2

    @pl.when(i == 0)
    def _():
        uold[...] = jnp.zeros_like(uold)
        sold[...] = jnp.zeros_like(sold)
        state[...] = jnp.zeros_like(state)

    aux = aux_ref[...]
    head_of = head_map(heads, channels)
    u = u_ref[...]
    s = s_ref[...]
    v = convolve(uext, u, uold[...], aux, vf_ref[...], vo_ref[...])
    ms = convolve(sext, s, sold[...], aux, sf_ref[...], so_ref[...])
    uold[...] = u[rows - 8 :, :]
    sold[...] = s[rows - 8 :, :]
    x = v * sigmoid(v)
    ms = ms * sigmoid(ms)
    into = ms[:, :half].astype(BF16)
    out_of = ms[:, half:].astype(BF16)
    lower = triangle(rows)
    tri = lower.astype(F32)
    _, steps, _, total, total_rows = decays(raw_ref[...], off_ref[...], dec_ref[...], tri)
    seg_col = aux[:, 6:7]
    seg_row = seg_ref[pl.ds(i, 1), :]
    previous = ends[i]
    last = ends[i + 1]
    far = jnp.where((seg_col == seg_row) & lower, 0.0, FAR)
    scores = nt(out_of, into)
    final = total[rows - 1 :, :]
    enter = jnp.exp(total) * (seg_col == previous).astype(F32)
    tail = jnp.exp(final - total) * (seg_col == last).astype(F32) * steps
    keep = jnp.exp(final) * jnp.where(last == previous, 1.0, 0.0)
    wide = spread(jnp.concatenate([steps, enter, tail, jnp.broadcast_to(keep, (8, heads)),
                                   jnp.broadcast_to(skip_ref[...], (8, heads))], axis=0), head_of)
    step_w = wide[:rows]
    enter_w = wide[rows : 2 * rows]
    tail_w = wide[2 * rows : 3 * rows]
    keep_w = wide[3 * rows : 3 * rows + 1]
    skip_w = wide[3 * rows + 8 : 3 * rows + 9]
    xs = x * step_w
    old = state[...]
    old_low = old.astype(BF16)
    kept_ref[0] = old_low
    carried = nn(out_of, old_low) * enter_w
    state[...] = old * keep_w + tn(into, (x * tail_w).astype(BF16))
    left = lax.broadcasted_iota(jnp.int32, (rows, 128), 1) < 64
    base = carried + skip_w * x
    silu_gate = gate_ref[...]
    silu_gate = silu_gate * sigmoid(silu_gate)
    square = jnp.zeros((rows, 128), F32)
    along = jnp.zeros((rows, 128), F32)
    for pair in range(heads // 2):
        lanes = slice(128 * pair, 128 * pair + 128)
        parts = []
        for h in (2 * pair, 2 * pair + 1):
            gap = (total[:, h : h + 1] - total_rows[h : h + 1, :]) + far
            parts.append((jnp.exp(gap) * scores).astype(BF16))
        xp = xs[:, lanes]
        stacked = jnp.concatenate([jnp.where(left, xp, 0.0), jnp.where(left, 0.0, xp)], axis=0)
        inside = nn(jnp.concatenate(parts, axis=1), stacked.astype(BF16))
        y = inside + base[:, lanes]
        y_ref[:, lanes] = y
        gated = y * silu_gate[:, lanes]
        square = square + gated * gated
        along = along + bg_ref[:, lanes] * ig_ref[:, lanes] * gated
    ones = jnp.ones((8, 128), BF16)
    for index, part in enumerate((square, along)):
        upper, low_part = halves(part)
        sum_ref[index : index + 1, :] = (nt(ones, upper) + nt(ones, low_part))[0:1, :]


def backward_kernel(
    ends,
    aux_ref,
    seg_ref,
    u_ref,
    s_ref,
    raw_ref,
    dy_ref,
    kept_ref,
    vf_ref,
    vo_ref,
    sf_ref,
    so_ref,
    off_ref,
    dec_ref,
    skip_ref,
    ubef_ref,
    sbef_ref,
    du_ref,
    ds_ref,
    dl_ref,
    draw_ref,
    chan_ref,
    maps_ref,
    head_ref,
    uext,
    sext,
    gext,
    hext,
    glater,
    hlater,
    dstate,
):
    j = pl.program_id(0)
    i = pl.num_programs(0) - 1 - j
    rows, channels = u_ref.shape
    heads = raw_ref.shape[1]
    half = s_ref.shape[1] // 2

    @pl.when(j == 0)
    def _():
        glater[...] = jnp.zeros_like(glater)
        hlater[...] = jnp.zeros_like(hlater)
        maps_ref[...] = jnp.zeros_like(maps_ref)
        dstate[...] = jnp.zeros_like(dstate)
        chan_ref[...] = jnp.zeros_like(chan_ref)
        head_ref[...] = jnp.zeros_like(head_ref)

    aux = aux_ref[...]
    head_of = head_map(heads, channels)
    u = u_ref[...]
    s = s_ref[...]
    first = jnp.where(i == 0, 0.0, 1.0)
    v = convolve(uext, u, ubef_ref[...] * first, aux, vf_ref[...], vo_ref[...])
    ms = convolve(sext, s, sbef_ref[...] * first, aux, sf_ref[...], so_ref[...])
    sig = sigmoid(v)
    x = v * sig
    state_sig = sigmoid(ms)
    ms = ms * state_sig
    into = ms[:, :half].astype(BF16)
    out_of = ms[:, half:].astype(BF16)
    lower = triangle(rows)
    tri = lower.astype(F32)
    moved, steps, rates, total, total_rows = decays(raw_ref[...], off_ref[...], dec_ref[...], tri)
    seg_col = aux[:, 6:7]
    seg_row = seg_ref[pl.ds(i, 1), :]
    previous = ends[i]
    last = ends[i + 1]
    far = jnp.where((seg_col == seg_row) & lower, 0.0, FAR)
    scores = nt(out_of, into)
    final = total[rows - 1 :, :]
    enter = jnp.exp(total) * (seg_col == previous).astype(F32)
    fade = jnp.exp(final - total) * (seg_col == last).astype(F32)
    keep = jnp.exp(final) * jnp.where(last == previous, 1.0, 0.0)
    wide = spread(jnp.concatenate([steps, enter, fade * steps, jnp.broadcast_to(keep, (8, heads)),
                                   jnp.broadcast_to(skip_ref[...], (8, heads))], axis=0), head_of)
    step_w = wide[:rows]
    enter_w = wide[rows : 2 * rows]
    tail_w = wide[2 * rows : 3 * rows]
    keep_w = wide[3 * rows : 3 * rows + 1]
    skip_w = wide[3 * rows + 8 : 3 * rows + 9]
    xs = x * step_w
    dy = dy_ref[...]
    old_low = kept_ref[0]
    after = dstate[...]
    after_low = after.astype(BF16)
    entered = (dy * enter_w).astype(BF16)
    carried = nn(out_of, old_low) * enter_w
    pushed = nn(into, after_low)
    tailed = (x * tail_w).astype(BF16)
    d_out = nt(entered, old_low)
    d_in = nt(tailed, after_low)
    kept_sum = jnp.sum(after * old_low.astype(F32), axis=0, keepdims=True) * keep_w
    dstate[...] = after * keep_w + tn(out_of, entered)
    left = lax.broadcasted_iota(jnp.int32, (rows, 128), 1) < 64
    d_scores = jnp.zeros((rows, rows), F32)
    row_sums = []
    col_sums = []
    pieces = []
    for pair in range(heads // 2):
        lanes = slice(128 * pair, 128 * pair + 128)
        xp = xs[:, lanes].astype(BF16)
        dp = dy[:, lanes]
        d_parts = [jnp.where(left, dp, 0.0).astype(BF16), jnp.where(left, 0.0, dp).astype(BF16)]
        parts = []
        for side in range(2):
            h = 2 * pair + side
            decay = jnp.exp((total[:, h : h + 1] - total_rows[h : h + 1, :]) + far)
            weight = decay * scores
            d_weight = nt(d_parts[side], xp)
            d_scores = d_scores + d_weight * decay
            grown = d_weight * weight
            row_sums.append(jnp.sum(grown, axis=1, keepdims=True))
            col_sums.append(jnp.sum(grown, axis=0, keepdims=True))
            parts.append(weight.astype(BF16))
        pieces.append(tn(jnp.concatenate(parts, axis=0), jnp.concatenate(d_parts, axis=0)))
    dxs = jnp.concatenate(pieces, axis=1)
    d_scores = d_scores.astype(BF16)
    d_maps = jnp.concatenate([d_in + tn(d_scores, out_of), d_out + nn(d_scores, into)], axis=1)
    d_maps = d_maps * (state_sig + ms * (1.0 - state_sig))
    ds_ref[...], dl_ref[...] = halves(unfilter(hext, hlater, maps_ref, d_maps, s, aux, sf_ref[...]))
    dx = dxs * step_w + pushed * tail_w + dy * skip_w
    by_step = gather(dxs * x, head_of)
    by_tail = gather(pushed * x, head_of)
    by_enter = gather(dy * carried, head_of)
    kept_head = gather(jnp.broadcast_to(kept_sum, (8, channels)), head_of)[0:1, :]
    tail_term = by_tail * fade * steps
    d_rows = jnp.concatenate(row_sums, axis=1) + by_enter - tail_term
    d_cols = jnp.concatenate(col_sums, axis=0)
    whole = jnp.sum(tail_term, axis=0, keepdims=True) + kept_head
    d_rates = tn(tri, d_rows, HIGH) - lax.dot_general(
        tri, d_cols, (((0,), (1,)), ((), ())), precision=HIGH, preferred_element_type=F32
    ) + whole
    rate_scale = -jnp.exp(dec_ref[...])
    d_steps = by_step + by_tail * fade + d_rates * rate_scale
    d_raw = d_steps * sigmoid(moved)
    draw_ref[...] = d_raw.astype(BF16)
    head_ref[0:1, :] += jnp.sum(d_raw, axis=0, keepdims=True)
    head_ref[1:2, :] += jnp.sum(d_rates * rates, axis=0, keepdims=True)
    dv = dx * (sig + x * (1.0 - sig))
    du = unfilter(gext, glater, chan_ref, dv, u, aux, vf_ref[...])
    chan_ref[5:6, :] += jnp.sum(dy * x, axis=0, keepdims=True)
    du_ref[...] = du.astype(BF16)


def side_columns(segment):
    cols = []
    for back in range(1, CONV):
        earlier = jnp.pad(segment, (back, 0), constant_values=-2)[:-back]
        cols.append((earlier == segment).astype(F32))
    for back in range(1, CONV):
        later = jnp.pad(segment, (0, back), constant_values=-2)[back:]
        cols.append((later == segment).astype(F32))
    cols.append(segment.astype(F32))
    cols.append(jnp.zeros_like(cols[0]))
    rows = segment.astype(F32).reshape(-1, CHUNK)
    ends = jnp.concatenate([jnp.full((1,), -3.0, F32), rows[:, -1]])
    return jnp.stack(cols, axis=1), rows, ends


def scan_forward(ends, aux, seg_rows, u, s, raw, gate, bg, vf, vo, sf, so, off, dec, skip, ig):
    length, channels = u.shape
    wide = s.shape[1]
    heads = raw.shape[1]
    half = wide // 2
    blocks = length // CHUNK

    def rowed(n):
        return pl.BlockSpec((CHUNK, n), lambda i: (i, 0))

    def whole(a):
        return pl.BlockSpec(a.shape, lambda i: (0, 0))

    return pl.pallas_call(
        forward_kernel,
        name="scan_forward",
        cost_estimate=pl.CostEstimate(
            flops=16 * length * channels * (CHUNK + half),
            transcendentals=length * (heads * CHUNK + 3 * channels),
            bytes_accessed=4 * length * (4 * channels + 2 * wide),
        ),
        grid=(blocks,),
        in_specs=[
            pl.BlockSpec(memory_space=pltpu.SMEM),
            rowed(8),
            whole(seg_rows),
            rowed(channels),
            rowed(wide),
            rowed(heads),
            rowed(channels),
            rowed(channels),
            *(whole(a) for a in (vf, vo, sf, so, off, dec, skip, ig)),
        ],
        out_specs=[
            rowed(channels),
            pl.BlockSpec((2, CHUNK), lambda i: (0, i)),
            pl.BlockSpec((1, half, channels), lambda i: (i, 0, 0)),
        ],
        out_shape=[
            jax.ShapeDtypeStruct((length, channels), F32),
            jax.ShapeDtypeStruct((2, length), F32),
            jax.ShapeDtypeStruct((blocks, half, channels), BF16),
        ],
        scratch_shapes=[
            pltpu.VMEM((CHUNK + 8, channels), F32),
            pltpu.VMEM((CHUNK + 8, wide), F32),
            pltpu.VMEM((8, channels), F32),
            pltpu.VMEM((8, wide), F32),
            pltpu.VMEM((half, channels), F32),
        ],
    )(ends, aux, seg_rows, u, s, raw, gate, bg, vf, vo, sf, so, off, dec, skip, ig)


def scan_backward(ends, aux, seg_rows, u, s, raw, dy, kept, vf, vo, sf, so, off, dec, skip):
    length, channels = u.shape
    wide = s.shape[1]
    heads = raw.shape[1]
    half = wide // 2
    blocks = length // CHUNK
    eighths = CHUNK // 8

    def rowed(n):
        return pl.BlockSpec((CHUNK, n), lambda j: (blocks - 1 - j, 0))

    def before(n):
        return pl.BlockSpec((8, n), lambda j: (jnp.maximum((blocks - 1 - j) * eighths - 1, 0), 0))

    def whole(a):
        return pl.BlockSpec(a.shape, lambda j: (0, 0))

    return pl.pallas_call(
        backward_kernel,
        name="scan_backward",
        cost_estimate=pl.CostEstimate(
            flops=40 * length * channels * (CHUNK + half),
            transcendentals=length * (heads * CHUNK + 3 * channels),
            bytes_accessed=4 * length * (4 * channels + 4 * wide),
        ),
        grid=(blocks,),
        in_specs=[
            pl.BlockSpec(memory_space=pltpu.SMEM),
            rowed(8),
            whole(seg_rows),
            rowed(channels),
            rowed(wide),
            rowed(heads),
            rowed(channels),
            pl.BlockSpec((1, half, channels), lambda j: (blocks - 1 - j, 0, 0)),
            *(whole(a) for a in (vf, vo, sf, so, off, dec, skip)),
            before(channels),
            before(wide),
        ],
        out_specs=[
            rowed(channels),
            rowed(wide),
            rowed(wide),
            rowed(heads),
            pl.BlockSpec((8, channels), lambda j: (0, 0)),
            pl.BlockSpec((8, wide), lambda j: (0, 0)),
            pl.BlockSpec((8, heads), lambda j: (0, 0)),
        ],
        out_shape=[
            jax.ShapeDtypeStruct((length, channels), BF16),
            jax.ShapeDtypeStruct((length, wide), BF16),
            jax.ShapeDtypeStruct((length, wide), BF16),
            jax.ShapeDtypeStruct((length, heads), BF16),
            jax.ShapeDtypeStruct((8, channels), F32),
            jax.ShapeDtypeStruct((8, wide), F32),
            jax.ShapeDtypeStruct((8, heads), F32),
        ],
        scratch_shapes=[
            pltpu.VMEM((CHUNK + 8, channels), F32),
            pltpu.VMEM((CHUNK + 8, wide), F32),
            pltpu.VMEM((CHUNK + 8, channels), F32),
            pltpu.VMEM((CHUNK + 8, wide), F32),
            pltpu.VMEM((8, channels), F32),
            pltpu.VMEM((8, wide), F32),
            pltpu.VMEM((half, channels), F32),
        ],
    )(ends, aux, seg_rows, u, s, raw, dy, kept, vf, vo, sf, so, off, dec, skip, u, s)


KINDS = {"O": "AAA", "G": "AAA", "X": "AAA"}
ORDER = (
    "*mo", "*mg", "G1", "O1", "O2", "G0", "O0", "G2", "G1", "*bwd", "*mx", "G1", "O2", "X2",
    "*grad", "O2", "*out", "G0+G1", "*state", "*tot", "X2", "X0", "G0", "O0+O2", "*pack", "X2",
    "X1", "X0+G0", "U", "R", "O2", "U", "O0", "U", "G2+X2", "E", "G1", "U", "F", "O1+O0", "E",
    "G2", "X2", "P", "G0", "F", "O1", "E", "X1+G2", "P", "F", "O0", "R", "P", "E", "O1", "X1",
    "E", "G2", "R", "F", "X0", "O1", "X1", "F", "O0", "O2", "G0", "G1", "G2", "X2", "X0", "X1",
    "P", "E", "O1", "F", "K", "X0", "R", "X1", "K", "K", "X0",
)


class Schedule:
    def __init__(self):
        self.groups = lax.axis_size("tensor")
        place = lax.axis_index("dp")
        self.rank = lax.axis_index("tensor")
        self.side = place & 1
        line = place >> 1
        self.end = (line == 0) | (line == 3)
        self.fold = ((place >> 1) ^ (place >> 2)) & 1
        self.route = {
            "pair": self.routes(lambda i: i ^ 1),
            "near": self.routes(lambda i: i ^ 2),
            "cross": self.routes(lambda i: i ^ 6),
            "middle": self.routes(lambda i: i ^ 6 if 2 <= i < 6 else None),
            "flip": self.routes(lambda i: None),
            "over": [
                (i * self.groups + j, i * self.groups + (j ^ 2))
                for i in range(8)
                for j in range(self.groups)
            ],
        }
        self.last = ()
        self.flows = {}
        self.done = {}

    def routes(self, target):
        pairs = []
        for i in range(8):
            to = target(i)
            for j in range(self.groups):
                there = i * self.groups + (j ^ 1) if to is None else to * self.groups + j
                pairs.append((i * self.groups + j, there))
        return pairs

    def hold(self, values):
        if self.last != ():
            values, self.last = lax.optimization_barrier((values, self.last))
        return values

    def add(self, name, flow):
        self.flows[name] = [flow, None]

    def step(self, names):
        arrived = [self.flows[name][1] for name in names]
        if all(value is not None for value in arrived):
            arrived = self.hold(arrived)
        asked = [self.flows[name][0].send(value) for name, value in zip(names, arrived)]
        if asked[0][0] == "done":
            self.done[names[0]] = asked[0][1]
            return
        route, value = asked[0]
        if len(names) == 2:
            value = jnp.where(self.end, value, asked[1][1])
        got = lax.ppermute(value, ("dp", "tensor"), self.route[route])
        self.last = (value,)
        for name in names:
            self.flows[name][1] = got

    def take(self, piece, which):
        rows = piece.shape[0] // 2
        return lax.dynamic_slice_in_dim(piece, which * rows, rows, 0)

    def join(self, half, other, which):
        return jnp.concatenate(
            [jnp.where(which == 0, half, other), jnp.where(which == 0, other, half)]
        )

    def cut(self, array, first, rows, which):
        return lax.dynamic_slice_in_dim(array, first + which * rows, rows, 0)

    def line_sum(self, array, first, rows):
        array = self.hold(array)
        half = self.cut(array, first, rows // 2, self.side)
        half = half + (yield "pair", self.cut(array, first, rows // 2, 1 - self.side))
        half = half + (yield "near", half)
        half = half + (yield "middle", half)
        half = jnp.where(self.end, (yield "near", half), half)
        yield "done", self.join(half, (yield "pair", half), self.side)

    def fold_sum(self, array, first, rows):
        array = self.hold(array)
        place = lax.axis_index("dp") >> 2
        half = self.cut(array, first, rows // 2, self.fold)
        half = half + (yield "near", self.cut(array, first, rows // 2, 1 - self.fold))
        part = self.take(half, place)
        part = part + (yield "cross", self.take(half, 1 - place))
        part = part + (yield "pair", part)
        half = self.join(part, (yield "cross", part), place)
        yield "done", self.join(half, (yield "near", half), self.fold)

    def scatter(self, array, axis):
        array = self.hold(array)
        size = array.shape[axis] // 4

        def part(which):
            return lax.dynamic_slice_in_dim(array, which * size, size, axis)

        far = yield "flip", part(self.rank ^ 3)
        near = yield "flip", part(self.rank ^ 1)
        over = yield "over", part(self.rank ^ 2) + far
        yield "done", part(self.rank) + near + over

    def gather(self, array):
        array = self.hold(array)
        rows = array.shape[0]
        other = yield "over", array
        pair = jnp.concatenate([array, other])
        crossed = yield "flip", pair
        full = jnp.zeros((4 * rows,) + array.shape[1:], array.dtype)
        for flip, value in zip((0, 2, 1, 3), (array, other, crossed[:rows], crossed[rows:])):
            full = lax.dynamic_update_slice_in_dim(full, value, (self.rank ^ flip) * rows, 0)
        yield "done", full


def on_device(
    tokens,
    segment,
    norm_gain,
    gate_weight,
    value_weight,
    state_weight,
    step_weight,
    value_filter,
    value_offset,
    state_filter,
    state_offset,
    step_offset,
    decay_log,
    skip_gain,
    inner_gain,
    output_weight,
    cotangent,
):
    groups = lax.axis_size("tensor")
    rank = lax.axis_index("tensor")
    channels = inner_gain.shape[0]
    inner_all = channels * groups
    heads = step_offset.shape[0]
    _, width = tokens.shape
    wide_states = state_weight.shape[1]
    cols = width // groups
    start = rank * cols
    cuts = width // channels

    wide = tokens.astype(F32)
    scale = lax.rsqrt(jnp.mean(wide * wide, axis=1, keepdims=True) + EPS)
    normed = (wide * scale * norm_gain[None, :]).astype(BF16)
    live = (segment >= 0).astype(F32)[:, None]
    masked = cotangent * live.astype(BF16)
    gate = nn(normed, gate_weight)
    values = nn(normed, value_weight)
    states = nn(normed, state_weight)
    raw = nn(normed, step_weight)
    branch_grad = nt(masked, output_weight)

    aux, seg_rows, ends = side_columns(segment)
    shared = (
        value_filter,
        value_offset[None, :],
        state_filter,
        state_offset[None, :],
        step_offset[None, :],
        decay_log[None, :],
        skip_gain[None, :],
    )
    scanned, sums, kept = scan_forward(
        ends, aux, seg_rows, values, states, raw, gate, branch_grad, *shared, inner_gain[None, :]
    )
    sums = lax.psum(sums, "tensor") / inner_all
    inner_scale = lax.rsqrt(sums[0] + EPS)
    pull = (inner_scale**3 * sums[1])[:, None]
    inner_scale = inner_scale[:, None]

    gate_sig = jax.nn.sigmoid(gate)
    silu_gate = gate * gate_sig
    gated = scanned * silu_gate
    unit_inner = gated * inner_scale
    branch = (unit_inner * inner_gain[None, :]).astype(BF16)
    gated_grad = inner_scale * (branch_grad * inner_gain[None, :]) - gated * pull
    gate_low = (gated_grad * scanned * (gate_sig + silu_gate * (1.0 - gate_sig))).astype(BF16)
    scanned_grad = gated_grad * silu_gate
    inner_gain_grad = jnp.sum(branch_grad * unit_inner, axis=0)
    env = {}

    def mo(hold):
        env["O"] = tn(branch, masked)
        return env["O"]

    def mg(hold):
        env["G"] = tn(normed, hold(gate_low))
        return env["G"]

    def bwd(hold):
        results = scan_backward(
            ends, aux, seg_rows, values, states, raw, hold(scanned_grad), kept, *shared
        )
        values_low, upper, lower, steps_low, by_channel, by_state, by_head = results
        env["low"] = (values_low, steps_low, upper, lower)
        env["sums"] = (by_channel, by_state, by_head)
        return values_low

    def mx(hold):
        env["X"] = tn(normed, hold(env["low"][0]))
        return env["X"]

    def grad(hold):
        values_low, steps_low, upper, lower = hold(env["low"])
        normed_grad = (
            nt(gate_low, gate_weight)
            + nt(steps_low, step_weight)
            + nt(upper, state_weight)
            + nt(lower, state_weight)
            + nt(values_low, value_weight)
        )
        env["R"] = normed_grad
        unit = hold(tokens).astype(F32) * scale
        env["along"] = jnp.sum(normed_grad * unit * norm_gain[None, :], axis=1)
        env["gain"] = jnp.sum(normed_grad * unit, axis=0)
        return normed_grad, env["along"], env["gain"]

    def state(hold):
        upper, lower = hold(env["low"][2:])
        env["U"] = tn(normed, upper) + tn(normed, lower)
        return env["U"]

    def out(hold):
        env["P"] = nn(hold(branch), output_weight)
        return env["P"]

    def tot(hold):
        env["along"], env["gain"], env["maps"] = lax.psum(
            hold((env["along"], env["gain"], env["sums"][1])), "tensor"
        )
        return env["along"], env["gain"], env["maps"]

    def rows_of(*items):
        laid = []
        for item in items:
            laid.append(jnp.pad(item, ((0, -item.shape[0] % 8), (0, channels - item.shape[1]))))
        return laid

    def pack(hold):
        by_channel, _, by_head = env["sums"]
        skip_part = jnp.sum(by_channel[5].reshape(heads, -1), axis=1)
        small = rows_of(
            by_channel,
            inner_gain_grad[None, :],
            hold(env["maps"]),
            jnp.stack([by_head[0], by_head[1], skip_part]),
        )
        step_grad = tn(env["low"][1], normed)
        for item in (env["gain"][None, :], step_grad):
            small.extend(rows_of(*(item[:, i * channels :][:, :channels] for i in range(cuts))))
        env["heights"] = [item.shape[0] for item in small]
        room = -sum(env["heights"]) % 16
        env["E"] = jnp.concatenate(small + [jnp.zeros((room, channels), F32)])
        return env["E"]

    def mixed_of(summed):
        token_share = lax.dynamic_slice_in_dim(tokens, start, cols, 1).astype(F32)
        return (token_share + live * summed).astype(BF16)

    def tokens_of(share_grad):
        unit_share = lax.dynamic_slice_in_dim(tokens, start, cols, 1).astype(F32) * scale
        gain_share = lax.dynamic_slice_in_dim(norm_gain, start, cols, 0)
        cotangent_share = lax.dynamic_slice_in_dim(cotangent, start, cols, 1).astype(F32)
        return cotangent_share + scale * (
            share_grad * gain_share[None, :] - unit_share * (env["along"] / width)[:, None]
        )

    tasks = dict(mo=mo, mg=mg, bwd=bwd, mx=mx, grad=grad, state=state, out=out, tot=tot, pack=pack)
    if lax.axis_size("dp") != 8 or groups != 4:
        for task in tasks.values():
            task(lambda value: value)
        mixed = mixed_of(lax.psum_scatter(env["P"], "tensor", scatter_dimension=1, tiled=True))
        shared_grad = lax.psum_scatter(env["R"], "tensor", scatter_dimension=1, tiled=True)
        tokens_grad = tokens_of(shared_grad)
        part = lax.psum_scatter(env["U"], "tensor", scatter_dimension=0, tiled=True)
        totals = lax.psum((env["O"], env["G"], env["X"], part, env["E"]), "dp")
        output_grad, gate_weight_grad, value_weight_grad, part, small = totals
        state_weight_grad = lax.all_gather(part, "tensor", axis=0, tiled=True)
    else:
        plan = Schedule()
        for entry in ORDER:
            if entry[0] == "*":
                result = tasks[entry[1:]](plan.hold)
                plan.last = result if isinstance(result, tuple) else (result,)
                continue
            names = entry.split("+")
            for name in names:
                if name in plan.flows:
                    continue
                if name in "PR":
                    flow = plan.scatter(env[name], 1)
                elif name == "U":
                    flow = plan.scatter(env[name], 0)
                elif name == "F":
                    flow = plan.line_sum(plan.done["U"], 0, plan.done["U"].shape[0])
                elif name == "K":
                    flow = plan.gather(plan.done["F"])
                elif name == "E":
                    flow = plan.line_sum(env["E"], 0, env["E"].shape[0])
                else:
                    kinds, array = KINDS[name[0]], env[name[0]]
                    rows, i = array.shape[0] // len(kinds), int(name[1])
                    flow = plan.line_sum if kinds[i] == "A" else plan.fold_sum
                    flow = flow(array, i * rows, rows)
                plan.add(name, flow)
            plan.step(names)
        mixed = mixed_of(plan.done["P"])
        tokens_grad = tokens_of(plan.done["R"])
        state_weight_grad = plan.done["K"]
        output_grad, gate_weight_grad, value_weight_grad = (
            jnp.concatenate([plan.done[f"{key}{i}"] for i in range(len(KINDS[key]))])
            for key in "OGX"
        )
        small = plan.done["E"]
    parts = []
    for height in env["heights"]:
        parts.append(small[:height])
        small = small[height:]
    chan, inner_grad, state_pair, head = parts[:4]
    gain_grad = jnp.concatenate([part[0] for part in parts[4 : 4 + cuts]])
    step_grad = jnp.concatenate([part[:heads] for part in parts[4 + cuts :]], axis=1)
    state_pair = state_pair[:, :wide_states]
    off, dec, skip = (head[i, :heads] for i in range(3))
    return (
        mixed,
        tokens_grad,
        gain_grad,
        gate_weight_grad,
        value_weight_grad,
        state_weight_grad,
        step_grad.T,
        chan[:4],
        chan[4],
        state_pair[:4],
        state_pair[4],
        off,
        dec,
        skip,
        inner_grad[0],
        output_grad,
    )


def solution(mesh):
    tokens = P("dp", None)
    columns = P(None, "tensor")
    split = P("tensor")

    return jax.shard_map(
        on_device,
        mesh=mesh,
        in_specs=(
            tokens,
            P("dp"),
            P(),
            columns,
            columns,
            P(),
            columns,
            columns,
            split,
            P(),
            P(),
            split,
            split,
            split,
            split,
            P("tensor", None),
            tokens,
        ),
        out_specs=(
            P("dp", "tensor"),
            P("dp", "tensor"),
            P(),
            columns,
            columns,
            P(),
            columns,
            columns,
            split,
            P(),
            P(),
            split,
            split,
            split,
            split,
            P("tensor", None),
        ),
        check_vma=False,
    )
```

profile of v0, /device:TPU:0, one launch (start us, length us, event | category | flops | bytes accessed | tf_op | source)
XLA Modules:
  0.0 473.2 jit_solution(15946871307069835586)
XLA Ops:
  27.6 12.8 %scan_forward.1 = (f32[1024,768]{1,0:T(8,128)}, f32[2,1024]{1,0:T(2,128)}, bf16[8,128,768]{2,1,0:T(8,128)(2,1)}) custom-call(f32[9]{0:T(128)} %pad_maximum_fusion.3.ends, f32[1024,8]{1,0:T(8,128)} %copy.44.aux_ref, f32[8,128]{1,0:T(8,128)} %copy-done.28, f32[1024,768]{1,0:T(8,128)} %fusion.43.u_ref.ubef_ref, f32[1024,256]{1,0:T(8,128)} %fusion.44.s_ref.sbef_ref, ...), custom_call_target="tpu_custom_call" | custom-call | flops 3221225472 | bytes 14680064 | tf_op jit(solution)/shard_map/scan_forward/pallas_call | solution.py:384
  40.5 9.1 %psum.28 = f32[2,1024]{1,0:T(2,128)S(1)} all-reduce(f32[2,1024]{1,0:T(2,128)} %get-tuple-element.108), channel_id=1, replica_groups=mesh['dp'=8,'tensor'=4] {'tensor'}, use_global_device_ids=true, to_apply=%region_1.2 | all-reduce | flops 2048 | bytes 16384 | tf_op jit(solution)/shard_map/psum | solution.py:672
  49.6 6.4 %fusion.14 = (f32[1024,768]{1,0:T(8,128)}, bf16[1024,768]{1,0:T(8,128)(2,1)S(1)}, f32[768]{0:T(1024)S(1)}, bf16[1024,768]{1,0:T(8,128)(2,1)S(1)}) fusion(f32[1024]{0:T(1024)S(1)} %fusion.23, f32[1024,768]{1,0:T(8,128)} %fusion.6.bg_ref, f32[768]{0:T(1024)S(1)} %copy-done.27, f32[1024]{0:T(1024)S(1)} %bitcast.66, f32[1024,768]{1,0:T(8,128)} %get-tuple-element.107, ...), kind=kLoop, calls=%fused_computation.29 | loop fusion | flops 16514304 | bytes 15742976 | tf_op jit(solution)/shard_map/mul | solution.py:684
  84.2 6.0 %fusion.49 = f32[1024,1536]{1,0:T(8,128)} fusion(bf16[1024,768]{1,0:T(8,128)(2,1)} %copy-done.14, bf16[1536,768]{1,0:T(8,128)(2,1)S(1)} %copy-done), kind=kOutput, calls=%fused_computation.175 | convolution fusion | flops 2415919104 | bytes 10223616 | tf_op jit(solution)/shard_map/dot_general | solution.py:25
  93.9 28.8 %scan_backward.1 = (bf16[1024,768]{1,0:T(8,128)(2,1)}, bf16[1024,256]{1,0:T(8,128)(2,1)}, bf16[1024,256]{1,0:T(8,128)(2,1)}, bf16[1024,12]{1,0:T(8,128)(2,1)}, f...) custom-call(f32[9]{0:T(128)} %pad_maximum_fusion.3.ends, f32[1024,8]{1,0:T(8,128)} %copy.44.aux_ref, ...), custom_call_target="tpu_custom_call" | custom-call | flops 8053063680 | bytes 16777216 | tf_op jit(solution)/shard_map/scan_backward/pallas_call | solution.py:441
  151.3 11.7 %fusion.3 = (f32[1536]{0:T(1024)S(1)}, f32[1024]{0:T(1024)S(1)}, f32[1024,1536]{1,0:T(8,128)}) fusion(bf16[1024,1536]{1,0:T(8,128)(2,1)} %param.17, f32[1024]{0:T(1024)S(1)} %add_rsqrt_fusion, f32[1536]{0:T(1024)S(1)} %copy-done.25, f32[1024,1536]{1,0:T(8,128)} %fusion.52, bf16[1024,256]{1,0:T(8,128)(2,1)} %get-tuple-element.137, ...), kind=kOutput, calls=%fused_computation.8 | convolution fusion | flops 821032448 | bytes 35934208 | tf_op jit(solution)/shard_map/dot_general | solution.py:25
  165.8 6.1 %fusion.53 = f32[1024,1536]{1,0:T(8,128)} fusion(bf16[1024,768]{1,0:T(8,128)(2,1)S(1)} %copy-done.7, bf16[768,1536]{1,0:T(8,128)(2,1)} %param.32), kind=kOutput, calls=%fused_computation.179 | convolution fusion | flops 2415919104 | bytes 10223616 | tf_op jit(solution)/shard_map/dot_general | solution.py:19
  178.5 11.8 %all-reduce.13 = (f32[1024]{0:T(1024)S(1)}, f32[1536]{0:T(1024)S(1)}, f32[8,256]{1,0:T(8,128)S(1)}) all-reduce(f32[1024]{0:T(1024)S(1)} %get-tuple-element.138, f32[1536]{0:T(1024)S(1)} %get-tuple-element.139, f32[8,256]{1,0:T(8,128)S(1)} %copy-done.30), channel_id=1, replica_groups=mesh['dp'=8,'tensor'=4] {'tensor'}, use_global_device_ids=true, to_apply=%region_4.5 | all-reduce | flops 4608 | bytes 36864 | tf_op jit(solution)/shard_map/psum | solution.py:734
  202.5 9.7 %collective-permute-done.8 = f32[256,768]{1,0:T(8,128)S(1)} collective-permute-done((f32[256,768]{1,0:T(8,128)S(1)}, f32[256,768]{1,0:T(8,128)S(1)}, u32[]{:S(2)}, u32[]{:S(2)}) %collective-permute-start.8) | collective-permute-done | bytes 786464 | tf_op jit(solution)/shard_map/ppermute | solution.py:557
  216.3 11.7 %collective-permute-done.16 = f32[128,1536]{1,0:T(8,128)S(1)} collective-permute-done((f32[128,1536]{1,0:T(8,128)S(1)}, f32[128,1536]{1,0:T(8,128)S(1)}, u32[]{:S(2)}, u32[]{:S(2)}) %collective-permute-start.16) | collective-permute-done | bytes 786464 | tf_op jit(solution)/shard_map/ppermute | solution.py:557
  247.5 15.9 %collective-permute-done.18 = f32[40,768]{1,0:T(8,128)S(1)} collective-permute-done((f32[40,768]{1,0:T(8,128)S(1)}, f32[40,768]{1,0:T(8,128)S(1)}, u32[]{:S(2)}, u32[]{:S(2)}) %collective-permute-start.18) | collective-permute-done | bytes 122912 | tf_op jit(solution)/shard_map/ppermute | solution.py:557
  274.9 10.9 %collective-permute-done.29 = f32[192,256]{1,0:T(8,128)S(1)} collective-permute-done((f32[192,256]{1,0:T(8,128)S(1)}, f32[192,256]{1,0:T(8,128)S(1)}, u32[]{:S(2)}, u32[]{:S(2)}) %collective-permute-start.29) | collective-permute-done | bytes 196640 | tf_op jit(solution)/shard_map/ppermute | solution.py:557
  298.8 7.5 %collective-permute-done.25 = f32[256,768]{1,0:T(8,128)S(1)} collective-permute-done((f32[256,768]{1,0:T(8,128)S(1)}, f32[256,768]{1,0:T(8,128)S(1)}, u32[]{:S(2)}, u32[]{:S(2)}) %collective-permute-start.25) | collective-permute-done | bytes 786464 | tf_op jit(solution)/shard_map/ppermute | solution.py:557
  306.9 16.3 %collective-permute-done.49 = f32[256,768]{1,0:T(8,128)S(1)} collective-permute-done((f32[256,768]{1,0:T(8,128)S(1)}, f32[256,768]{1,0:T(8,128)S(1)}, u32[]{:S(2)}, u32[]{:S(2)}) %collective-permute-start.49) | collective-permute-done | bytes 786464 | tf_op jit(solution)/shard_map/ppermute | solution.py:557
  323.5 13.4 %collective-permute-done.54 = f32[256,768]{1,0:T(8,128)S(1)} collective-permute-done((f32[256,768]{1,0:T(8,128)S(1)}, f32[256,768]{1,0:T(8,128)S(1)}, u32[]{:S(2)}, u32[]{:S(2)}) %collective-permute-start.54) | collective-permute-done | bytes 786464 | tf_op jit(solution)/shard_map/ppermute | solution.py:557
  344.2 9.2 %collective-permute-done.32 = f32[256,768]{1,0:T(8,128)S(1)} collective-permute-done((f32[256,768]{1,0:T(8,128)S(1)}, f32[256,768]{1,0:T(8,128)S(1)}, u32[]{:S(2)}, u32[]{:S(2)}) %collective-permute-start.32) | collective-permute-done | bytes 786464 | tf_op jit(solution)/shard_map/ppermute | solution.py:557
  353.4 6.6 %collective-permute-start.43 = (f32[40,768]{1,0:T(8,128)S(1)}, f32[40,768]{1,0:T(8,128)S(1)}, u32[]{:S(2)}, u32[]{:S(2)}) collective-permute-start(f32[40,768]{1,0:T(8,128)S(1)} %add.407), channel_id=1, source_target_pairs={{0,8},{1,9},{2,10},{3,11},{4,12},{5,13},{6,14},{7,15},{8,0},{9,1},... | collective-permute-start | bytes 368648 | tf_op jit(solution)/shard_map/ppermute | solution.py:557
  369.3 10.6 %collective-permute-start.36 = (f32[128,1536]{1,0:T(8,128)S(1)}, f32[128,1536]{1,0:T(8,128)S(1)}, u32[]{:S(2)}, u32[]{:S(2)}) collective-permute-start(f32[128,1536]{1,0:T(8,128)S(1)} %add.408), channel_id=1, source_target_pairs={{0,8},{1,9},{2,10},{3,11},{4,12},{5,13},{6,14},{7,15},{8,0},{9,1},... | collective-permute-start | bytes 2359304 | tf_op jit(solution)/shard_map/ppermute | solution.py:557
  384.1 14.2 %collective-permute-done.36 = f32[128,1536]{1,0:T(8,128)S(1)} collective-permute-done((f32[128,1536]{1,0:T(8,128)S(1)}, f32[128,1536]{1,0:T(8,128)S(1)}, u32[]{:S(2)}, u32[]{:S(2)}) %collective-permute-start.36) | collective-permute-done | bytes 786464 | tf_op jit(solution)/shard_map/ppermute | solution.py:557
  404.9 15.3 %collective-permute-done.51 = f32[256,768]{1,0:T(8,128)S(1)} collective-permute-done((f32[256,768]{1,0:T(8,128)S(1)}, f32[256,768]{1,0:T(8,128)S(1)}, u32[]{:S(2)}, u32[]{:S(2)}) %collective-permute-start.51) | collective-permute-done | bytes 786464 | tf_op jit(solution)/shard_map/ppermute | solution.py:557
  428.2 9.7 %collective-permute-done.55 = f32[384,256]{1,0:T(8,128)S(1)} collective-permute-done((f32[384,256]{1,0:T(8,128)S(1)}, f32[384,256]{1,0:T(8,128)S(1)}, u32[]{:S(2)}, u32[]{:S(2)}) %collective-permute-start.55) | collective-permute-done | bytes 393248 | tf_op jit(solution)/shard_map/ppermute | solution.py:557
  438.9 5.9 %collective-permute-done.58 = f32[128,1536]{1,0:T(8,128)S(1)} collective-permute-done((f32[128,1536]{1,0:T(8,128)S(1)}, f32[128,1536]{1,0:T(8,128)S(1)}, u32[]{:S(2)}, u32[]{:S(2)}) %collective-permute-start.58) | collective-permute-done | bytes 786464 | tf_op jit(solution)/shard_map/ppermute | solution.py:557
  450.8 10.9 %collective-permute-done.52 = f32[256,768]{1,0:T(8,128)S(1)} collective-permute-done((f32[256,768]{1,0:T(8,128)S(1)}, f32[256,768]{1,0:T(8,128)S(1)}, u32[]{:S(2)}, u32[]{:S(2)}) %collective-permute-start.52) | collective-permute-done | bytes 786464 | tf_op jit(solution)/shard_map/ppermute | solution.py:557
  462.0 8.3 %collective-permute-done.53 = f32[256,768]{1,0:T(8,128)S(1)} collective-permute-done((f32[256,768]{1,0:T(8,128)S(1)}, f32[256,768]{1,0:T(8,128)S(1)}, u32[]{:S(2)}, u32[]{:S(2)}) %collective-permute-start.53) | collective-permute-done | bytes 786464 | tf_op jit(solution)/shard_map/ppermute | solution.py:557
  (339 shorter events, 202.1 us)
Async XLA Ops:
  70.6 172.8 %collective-permute-start.19 = (f32[128,1536]{1,0:T(8,128)}, f32[128,1536]{1,0:T(8,128)}, u32[]{:S(2)}, u32[]{:S(2)}) collective-permute-start(f32[128,1536]{1,0:T(8,128)} %constant_dynamic-slice_fusion.15), channel_id=1, source_target_pairs={{0,4},{1,5},{2,6},{3,7},{4,0},{5,1},{6,2},{7,3},{8,12},{9,13},{10,... | collective-permute-start | bytes 2359304 | tf_op jit(solution)/shard_map/ppermute | solution.py:557
  73.2 65.0 %collective-permute-start = (f32[128,1536]{1,0:T(8,128)}, f32[128,1536]{1,0:T(8,128)}, u32[]{:S(2)}, u32[]{:S(2)}) collective-permute-start(f32[128,1536]{1,0:T(8,128)} %constant_dynamic-slice_fusion.14), channel_id=1, source_target_pairs={{0,4},{1,5},{2,6},{3,7},{4,0},{5,1},{6,2},{7,3},{8,12},{9,13},{10,... | collective-permute-start | bytes 2359304 | tf_op jit(solution)/shard_map/ppermute | solution.py:557
  76.8 95.2 %collective-permute-start.6 = (f32[256,768]{1,0:T(8,128)}, f32[256,768]{1,0:T(8,128)}, u32[]{:S(2)}, u32[]{:S(2)}) collective-permute-start(f32[256,768]{1,0:T(8,128)} %constant_dynamic-slice_fusion.13), channel_id=1, source_target_pairs={{0,4},{1,5},{2,6},{3,7},{4,0},{5,1},{6,2},{7,3},{8,12},{9,13},{10,... | collective-permute-start | bytes 2359304 | tf_op jit(solution)/shard_map/ppermute | solution.py:557
  79.3 118.8 %collective-permute-start.9 = (f32[128,1536]{1,0:T(8,128)}, f32[128,1536]{1,0:T(8,128)}, u32[]{:S(2)}, u32[]{:S(2)}) collective-permute-start(f32[128,1536]{1,0:T(8,128)} %constant_dynamic-slice_fusion.12), channel_id=1, source_target_pairs={{0,4},{1,5},{2,6},{3,7},{4,0},{5,1},{6,2},{7,3},{8,12},{9,13},{10,... | collective-permute-start | bytes 2359304 | tf_op jit(solution)/shard_map/ppermute | solution.py:557
  92.3 42.2 %collective-permute-start.2 = (f32[256,768]{1,0:T(8,128)}, f32[256,768]{1,0:T(8,128)}, u32[]{:S(2)}, u32[]{:S(2)}) collective-permute-start(f32[256,768]{1,0:T(8,128)} %dynamic-slice_add_fusion.9), channel_id=1, source_target_pairs={{0,8},{1,9},{2,10},{3,11},{4,12},{5,13},{6,14},{7,15},{8,0},{9,1},... | collective-permute-start | bytes 2359304 | tf_op jit(solution)/shard_map/ppermute | solution.py:557
  138.2 33.8 %collective-permute-start.7 = (f32[256,768]{1,0:T(8,128)}, f32[256,768]{1,0:T(8,128)}, u32[]{:S(2)}, u32[]{:S(2)}) collective-permute-start(f32[256,768]{1,0:T(8,128)} %add.360), channel_id=1, source_target_pairs={{0,1},{1,0},{2,3},{3,2},{4,5},{5,4},{6,7},{7,6},{8,16},{9,17},{10,... | collective-permute-start | bytes 2359304 | tf_op jit(solution)/shard_map/ppermute | solution.py:557
  163.0 27.3 %collective-permute-start.5 = (f32[256,768]{1,0:T(8,128)}, f32[256,768]{1,0:T(8,128)}, u32[]{:S(2)}, u32[]{:S(2)}) collective-permute-start(f32[256,768]{1,0:T(8,128)} %constant_dynamic-slice_fusion.10), channel_id=1, source_target_pairs={{0,4},{1,5},{2,6},{3,7},{4,0},{5,1},{6,2},{7,3},{8,12},{9,13},{10,... | collective-permute-start | bytes 2359304 | tf_op jit(solution)/shard_map/ppermute | solution.py:557
  200.5 27.5 %collective-permute-start.16 = (f32[128,1536]{1,0:T(8,128)S(1)}, f32[128,1536]{1,0:T(8,128)S(1)}, u32[]{:S(2)}, u32[]{:S(2)}) collective-permute-start(f32[128,1536]{1,0:T(8,128)S(1)} %get-tuple-element.214), channel_id=1, source_target_pairs={{0,8},{1,9},{2,10},{3,11},{4,12},{5,13},{6,14},{7,15},{8,0},{9,1},... | collective-permute-start | bytes 2359304 | tf_op jit(solution)/shard_map/ppermute | solution.py:557
  228.0 68.5 %collective-permute-start.39 = (f32[1024,384]{1,0:T(8,128)S(1)}, f32[1024,384]{1,0:T(8,128)S(1)}, u32[]{:S(2)}, u32[]{:S(2)}) collective-permute-start(f32[1024,384]{1,0:T(8,128)S(1)} %constant_dynamic-slice_fusion.6), channel_id=1, source_target_pairs={{0,1},{1,0},{2,3},{3,2},{4,5},{5,4},{6,7},{7,6},{8,9},{9,8},{10,11... | collective-permute-start | bytes 4718600 | tf_op jit(solution)/shard_map/ppermute | solution.py:557
  232.5 40.6 %collective-permute-start.30 = (f32[256,768]{1,0:T(8,128)S(1)}, f32[256,768]{1,0:T(8,128)S(1)}, u32[]{:S(2)}, u32[]{:S(2)}) collective-permute-start(f32[256,768]{1,0:T(8,128)S(1)} %get-tuple-element.212), channel_id=1, source_target_pairs={{0,8},{1,9},{2,10},{3,11},{4,12},{5,13},{6,14},{7,15},{8,0},{9,1},... | collective-permute-start | bytes 2359304 | tf_op jit(solution)/shard_map/ppermute | solution.py:557
  241.7 44.1 %collective-permute-start.59 = (f32[128,1536]{1,0:T(8,128)S(1)}, f32[128,1536]{1,0:T(8,128)S(1)}, u32[]{:S(2)}, u32[]{:S(2)}) collective-permute-start(f32[128,1536]{1,0:T(8,128)S(1)} %broadcast_select_fusion.3), channel_id=1, source_target_pairs={{0,4},{1,5},{2,6},{3,7},{4,0},{5,1},{6,2},{7,3},{8,12},{9,13},{10,... | collective-permute-start | bytes 2359304 | tf_op jit(solution)/shard_map/ppermute | solution.py:557
  292.7 30.5 %collective-permute-start.49 = (f32[256,768]{1,0:T(8,128)S(1)}, f32[256,768]{1,0:T(8,128)S(1)}, u32[]{:S(2)}, u32[]{:S(2)}) collective-permute-start(f32[256,768]{1,0:T(8,128)S(1)} %broadcast_select_fusion.9), channel_id=1, source_target_pairs={{0,4},{1,5},{2,6},{3,7},{4,0},{5,1},{6,2},{7,3},{8,12},{9,13},{10,... | collective-permute-start | bytes 2359304 | tf_op jit(solution)/shard_map/ppermute | solution.py:557
  298.0 42.3 %collective-permute-start.24 = (f32[1024,384]{1,0:T(8,128)S(1)}, f32[1024,384]{1,0:T(8,128)S(1)}, u32[]{:S(2)}, u32[]{:S(2)}) collective-permute-start(f32[1024,384]{1,0:T(8,128)S(1)} %get-tuple-element.225), channel_id=1, source_target_pairs={{0,1},{1,0},{2,3},{3,2},{4,5},{5,4},{6,7},{7,6},{8,9},{9,8},{10,11... | collective-permute-start | bytes 4718600 | tf_op jit(solution)/shard_map/ppermute | solution.py:557
  298.3 38.6 %collective-permute-start.54 = (f32[256,768]{1,0:T(8,128)S(1)}, f32[256,768]{1,0:T(8,128)S(1)}, u32[]{:S(2)}, u32[]{:S(2)}) collective-permute-start(f32[256,768]{1,0:T(8,128)S(1)} %broadcast_select_fusion.10), channel_id=1, source_target_pairs={{0,4},{1,5},{2,6},{3,7},{4,0},{5,1},{6,2},{7,3},{8,12},{9,13},{10,... | collective-permute-start | bytes 2359304 | tf_op jit(solution)/shard_map/ppermute | solution.py:557
  306.4 53.7 %collective-permute-start.23 = (f32[1024,384]{1,0:T(8,128)S(1)}, f32[1024,384]{1,0:T(8,128)S(1)}, u32[]{:S(2)}, u32[]{:S(2)}) collective-permute-start(f32[1024,384]{1,0:T(8,128)S(1)} %get-tuple-element.224), channel_id=1, source_target_pairs={{0,1},{1,0},{2,3},{3,2},{4,5},{5,4},{6,7},{7,6},{8,9},{9,8},{10,11... | collective-permute-start | bytes 4718600 | tf_op jit(solution)/shard_map/ppermute | solution.py:557
  306.4 37.6 %collective-permute-start.33 = (f32[128,1536]{1,0:T(8,128)S(1)}, f32[128,1536]{1,0:T(8,128)S(1)}, u32[]{:S(2)}, u32[]{:S(2)}) collective-permute-start(f32[128,1536]{1,0:T(8,128)S(1)} %fusion.21), channel_id=1, source_target_pairs={{0,1},{1,0},{2,3},{3,2},{4,5},{5,4},{6,7},{7,6},{8,16},{9,17},{10,... | collective-permute-start | bytes 2359304 | tf_op jit(solution)/shard_map/ppermute | solution.py:557
  338.9 87.3 %collective-permute-start.44 = (f32[1024,384]{1,0:T(8,128)S(1)}, f32[1024,384]{1,0:T(8,128)S(1)}, u32[]{:S(2)}, u32[]{:S(2)}) collective-permute-start(f32[1024,384]{1,0:T(8,128)S(1)} %get-tuple-element.223), channel_id=1, source_target_pairs={{0,2},{1,3},{2,0},{3,1},{4,6},{5,7},{6,4},{7,5},{8,10},{9,11},{10,... | collective-permute-start | bytes 4718600 | tf_op jit(solution)/shard_map/ppermute | solution.py:557
  342.4 60.4 %collective-permute-start.57 = (f32[128,1536]{1,0:T(8,128)S(1)}, f32[128,1536]{1,0:T(8,128)S(1)}, u32[]{:S(2)}, u32[]{:S(2)}) collective-permute-start(f32[128,1536]{1,0:T(8,128)S(1)} %broadcast_select_fusion.1), channel_id=1, source_target_pairs={{0,4},{1,5},{2,6},{3,7},{4,0},{5,1},{6,2},{7,3},{8,12},{9,13},{10,... | collective-permute-start | bytes 2359304 | tf_op jit(solution)/shard_map/ppermute | solution.py:557
  344.0 40.1 %collective-permute-start.42 = (f32[1024,384]{1,0:T(8,128)S(1)}, f32[1024,384]{1,0:T(8,128)S(1)}, u32[]{:S(2)}, u32[]{:S(2)}) collective-permute-start(f32[1024,384]{1,0:T(8,128)S(1)} %get-tuple-element.222), channel_id=1, source_target_pairs={{0,1},{1,0},{2,3},{3,2},{4,5},{5,4},{6,7},{7,6},{8,9},{9,8},{10,11... | collective-permute-start | bytes 4718600 | tf_op jit(solution)/shard_map/ppermute | solution.py:557
  360.1 40.3 %collective-permute-start.35 = (f32[256,768]{1,0:T(8,128)S(1)}, f32[256,768]{1,0:T(8,128)S(1)}, u32[]{:S(2)}, u32[]{:S(2)}) collective-permute-start(f32[256,768]{1,0:T(8,128)S(1)} %fusion.22), channel_id=1, source_target_pairs={{0,1},{1,0},{2,3},{3,2},{4,5},{5,4},{6,7},{7,6},{8,16},{9,17},{10,... | collective-permute-start | bytes 2359304 | tf_op jit(solution)/shard_map/ppermute | solution.py:557
  369.3 29.0 %collective-permute-start.36 = (f32[128,1536]{1,0:T(8,128)S(1)}, f32[128,1536]{1,0:T(8,128)S(1)}, u32[]{:S(2)}, u32[]{:S(2)}) collective-permute-start(f32[128,1536]{1,0:T(8,128)S(1)} %add.408), channel_id=1, source_target_pairs={{0,8},{1,9},{2,10},{3,11},{4,12},{5,13},{6,14},{7,15},{8,0},{9,1},... | collective-permute-start | bytes 2359304 | tf_op jit(solution)/shard_map/ppermute | solution.py:557
  400.4 38.5 %collective-permute-start.31 = (f32[1024,384]{1,0:T(8,128)S(1)}, f32[1024,384]{1,0:T(8,128)S(1)}, u32[]{:S(2)}, u32[]{:S(2)}) collective-permute-start(f32[1024,384]{1,0:T(8,128)S(1)} %dynamic-slice_add_fusion.1), channel_id=1, source_target_pairs={{0,2},{1,3},{2,0},{3,1},{4,6},{5,7},{6,4},{7,5},{8,10},{9,11},{10,... | collective-permute-start | bytes 4718600 | tf_op jit(solution)/shard_map/ppermute | solution.py:557
  426.3 35.4 %collective-permute-start.52 = (f32[256,768]{1,0:T(8,128)S(1)}, f32[256,768]{1,0:T(8,128)S(1)}, u32[]{:S(2)}, u32[]{:S(2)}) collective-permute-start(f32[256,768]{1,0:T(8,128)S(1)} %broadcast_select_fusion.5), channel_id=1, source_target_pairs={{0,4},{1,5},{2,6},{3,7},{4,0},{5,1},{6,2},{7,3},{8,12},{9,13},{10,... | collective-permute-start | bytes 2359304 | tf_op jit(solution)/shard_map/ppermute | solution.py:557
  438.3 32.1 %collective-permute-start.53 = (f32[256,768]{1,0:T(8,128)S(1)}, f32[256,768]{1,0:T(8,128)S(1)}, u32[]{:S(2)}, u32[]{:S(2)}) collective-permute-start(f32[256,768]{1,0:T(8,128)S(1)} %broadcast_select_fusion.7), channel_id=1, source_target_pairs={{0,4},{1,5},{2,6},{3,7},{4,0},{5,1},{6,2},{7,3},{8,12},{9,13},{10,... | collective-permute-start | bytes 2359304 | tf_op jit(solution)/shard_map/ppermute | solution.py:557
  (82 other events, 986.4 us)
where the time goes:
time: 482 us; the launch traced here: 473 us
  waiting for transfers between devices  181 us (38%)
  starting transfers between devices  75.6 us (16%)
  matrix products  64.7 us (13%)
  other arithmetic  53.8 us (11%)
  Pallas kernels  41.7 us (9%)
  local copies, waits for them, and re-layouts  33.7 us (7%)
  blocking collectives  20.9 us (4%)
    ppermute x60, waiting for transfers between devices, step(): got = lax.ppermute(value, ('dp', 'tensor'), self.route[route])  181 us
    ppermute x60, starting transfers between devices, step(): got = lax.ppermute(value, ('dp', 'tensor'), self.route[route])  75.6 us
    pallas_call x1, Pallas kernels, scan_backward(): pl.pallas_call(backward_kernel, name='scan_backward', cost_estimate=pl.Co...  28.8 us
    dot_general x6, matrix products, nt(): lax.dot_general(a, b, (((1,), (1,)), ((), ())), precision=precision, pref...  28.6 us
    dot_general x5, matrix products, nn(): lax.dot_general(a, b, (((1,), (0,)), ((), ())), precision=precision, pref...  18.3 us
    dot_general x6, matrix products, tn(): lax.dot_general(a, b, (((0,), (0,)), ((), ())), precision=precision, pref...  17.7 us
    dynamic_slice x11, local copies, waits for them, and re-layouts, cut(): return lax.dynamic_slice_in_dim(array, first + which * rows, rows, 0)  16.1 us
    pallas_call x1, Pallas kernels, scan_forward(): pl.pallas_call(forward_kernel, name='scan_forward', cost_estimate=pl.Cost...  12.8 us
  transfers between devices with their start and end apart: 60, of which 23 were waited for; matrix products, arithmetic and copies ran while one was open for 22% of the time, Pallas kernels for 6%

commit v1 on v0

--- a/solution.py
+++ b/solution.py
@@ -105,6 +105,80 @@
         rates, tri, (((0,), (1,)), ((), ())), precision=HIGH, preferred_element_type=F32
     )
     return moved, steps, rates, total, total_rows
+
+
+def front_kernel(
+    live_ref,
+    tokens_ref,
+    cot_ref,
+    gain_ref,
+    gate_w,
+    value_w,
+    state_w,
+    step_w,
+    out_w,
+    normed_ref,
+    gate_ref,
+    value_ref,
+    state_ref,
+    step_ref,
+    masked_ref,
+    bg_ref,
+):
+    wide = tokens_ref[...].astype(F32)
+    scale = lax.rsqrt(jnp.mean(wide * wide, axis=1, keepdims=True) + EPS)
+    normed = (wide * scale * gain_ref[...][None, :]).astype(BF16)
+    normed_ref[...] = normed
+    live = (live_ref[:, 6:7] >= 0.0).astype(F32)
+    masked = (cot_ref[...].astype(F32) * live).astype(BF16)
+    masked_ref[...] = masked
+    value_ref[...] = nn(normed, value_w[...])
+    state_ref[...] = nn(normed, state_w[...])
+    step_ref[...] = nt(normed, step_w[...])
+    gate_ref[...] = nn(normed, gate_w[...])
+    bg_ref[...] = nt(masked, out_w[...])
+
+
+def front(aux, tokens, cotangent, gain, gate_w, value_w, state_w, step_w, out_w):
+    length, width = tokens.shape
+    rows = 256
+    channels, wide, heads = gate_w.shape[1], state_w.shape[1], step_w.shape[0]
+
+    def rowed(n):
+        return pl.BlockSpec((rows, n), lambda i: (i, 0))
+
+    def whole(a):
+        return pl.BlockSpec(a.shape, lambda i: (0,) * a.ndim)
+
+    return pl.pallas_call(
+        front_kernel,
+        name="front",
+        grid=(length // rows,),
+        in_specs=[
+            rowed(8),
+            rowed(width),
+            rowed(width),
+            *(whole(a) for a in (gain, gate_w, value_w, state_w, step_w, out_w)),
+        ],
+        out_specs=[
+            rowed(width),
+            rowed(channels),
+            rowed(channels),
+            rowed(wide),
+            rowed(heads),
+            rowed(width),
+            rowed(channels),
+        ],
+        out_shape=[
+            jax.ShapeDtypeStruct((length, width), BF16),
+            jax.ShapeDtypeStruct((length, channels), F32),
+            jax.ShapeDtypeStruct((length, channels), F32),
+            jax.ShapeDtypeStruct((length, wide), F32),
+            jax.ShapeDtypeStruct((length, heads), F32),
+            jax.ShapeDtypeStruct((length, width), BF16),
+            jax.ShapeDtypeStruct((length, channels), F32),
+        ],
+    )(aux, tokens, cotangent, gain, gate_w, value_w, state_w, step_w, out_w)
 
 
 def forward_kernel(
@@ -148,8 +222,8 @@
     head_of = head_map(heads, channels)
     u = u_ref[...]
     s = s_ref[...]
-    v = convolve(uext, u, uold[...], aux, vf_ref[...], vo_ref[...])
-    ms = convolve(sext, s, sold[...], aux, sf_ref[...], so_ref[...])
+    v = convolve(uext, u, uold[...], aux, vf_ref[...], vo_ref[...][None, :])
+    ms = convolve(sext, s, sold[...], aux, sf_ref[...], so_ref[...][None, :])
     uold[...] = u[rows - 8 :, :]
     sold[...] = s[rows - 8 :, :]
     x = v * sigmoid(v)
@@ -158,7 +232,7 @@
     out_of = ms[:, half:].astype(BF16)
     lower = triangle(rows)
     tri = lower.astype(F32)
-    _, steps, _, total, total_rows = decays(raw_ref[...], off_ref[...], dec_ref[...], tri)
+    _, steps, _, total, total_rows = decays(raw_ref[...], off_ref[...][None, :], dec_ref[...][None, :], tri)
     seg_col = aux[:, 6:7]
     seg_row = seg_ref[pl.ds(i, 1), :]
     previous = ends[i]
@@ -170,7 +244,7 @@
     tail = jnp.exp(final - total) * (seg_col == last).astype(F32) * steps
     keep = jnp.exp(final) * jnp.where(last == previous, 1.0, 0.0)
     wide = spread(jnp.concatenate([steps, enter, tail, jnp.broadcast_to(keep, (8, heads)),
-                                   jnp.broadcast_to(skip_ref[...], (8, heads))], axis=0), head_of)
+                                   jnp.broadcast_to(skip_ref[...][None, :], (8, heads))], axis=0), head_of)
     step_w = wide[:rows]
     enter_w = wide[rows : 2 * rows]
     tail_w = wide[2 * rows : 3 * rows]
@@ -186,6 +260,7 @@
     base = carried + skip_w * x
     silu_gate = gate_ref[...]
     silu_gate = silu_gate * sigmoid(silu_gate)
+    ig = ig_ref[...][None, :]
     square = jnp.zeros((rows, 128), F32)
     along = jnp.zeros((rows, 128), F32)
     for pair in range(heads // 2):
@@ -201,7 +276,7 @@
         y_ref[:, lanes] = y
         gated = y * silu_gate[:, lanes]
         square = square + gated * gated
-        along = along + bg_ref[:, lanes] * ig_ref[:, lanes] * gated
+        along = along + bg_ref[:, lanes] * ig[:, lanes] * gated
     ones = jnp.ones((8, 128), BF16)
     for index, part in enumerate((square, along)):
         upper, low_part = halves(part)
@@ -261,8 +336,8 @@
     u = u_ref[...]
     s = s_ref[...]
     first = jnp.where(i == 0, 0.0, 1.0)
-    v = convolve(uext, u, ubef_ref[...] * first, aux, vf_ref[...], vo_ref[...])
-    ms = convolve(sext, s, sbef_ref[...] * first, aux, sf_ref[...], so_ref[...])
+    v = convolve(uext, u, ubef_ref[...] * first, aux, vf_ref[...], vo_ref[...][None, :])
+    ms = convolve(sext, s, sbef_ref[...] * first, aux, sf_ref[...], so_ref[...][None, :])
     sig = sigmoid(v)
     x = v * sig
     state_sig = sigmoid(ms)
@@ -271,7 +346,7 @@
     out_of = ms[:, half:].astype(BF16)
     lower = triangle(rows)
     tri = lower.astype(F32)
-    moved, steps, rates, total, total_rows = decays(raw_ref[...], off_ref[...], dec_ref[...], tri)
+    moved, steps, rates, total, total_rows = decays(raw_ref[...], off_ref[...][None, :], dec_ref[...][None, :], tri)
     seg_col = aux[:, 6:7]
     seg_row = seg_ref[pl.ds(i, 1), :]
     previous = ends[i]
@@ -283,7 +358,7 @@
     fade = jnp.exp(final - total) * (seg_col == last).astype(F32)
     keep = jnp.exp(final) * jnp.where(last == previous, 1.0, 0.0)
     wide = spread(jnp.concatenate([steps, enter, fade * steps, jnp.broadcast_to(keep, (8, heads)),
-                                   jnp.broadcast_to(skip_ref[...], (8, heads))], axis=0), head_of)
+                                   jnp.broadcast_to(skip_ref[...][None, :], (8, heads))], axis=0), head_of)
     step_w = wide[:rows]
     enter_w = wide[rows : 2 * rows]
     tail_w = wide[2 * rows : 3 * rows]
@@ -341,7 +416,7 @@
     d_rates = tn(tri, d_rows, HIGH) - lax.dot_general(
         tri, d_cols, (((0,), (1,)), ((), ())), precision=HIGH, preferred_element_type=F32
     ) + whole
-    rate_scale = -jnp.exp(dec_ref[...])
+    rate_scale = -jnp.exp(dec_ref[...][None, :])
     d_steps = by_step + by_tail * fade + d_rates * rate_scale
     d_raw = d_steps * sigmoid(moved)
     draw_ref[...] = d_raw.astype(BF16)
@@ -379,7 +454,7 @@
         return pl.BlockSpec((CHUNK, n), lambda i: (i, 0))
 
     def whole(a):
-        return pl.BlockSpec(a.shape, lambda i: (0, 0))
+        return pl.BlockSpec(a.shape, lambda i: (0,) * a.ndim)
 
     return pl.pallas_call(
         forward_kernel,
@@ -436,7 +511,7 @@
         return pl.BlockSpec((8, n), lambda j: (jnp.maximum((blocks - 1 - j) * eighths - 1, 0), 0))
 
     def whole(a):
-        return pl.BlockSpec(a.shape, lambda j: (0, 0))
+        return pl.BlockSpec(a.shape, lambda j: (0,) * a.ndim)
 
     return pl.pallas_call(
         backward_kernel,
@@ -490,14 +565,14 @@
     )(ends, aux, seg_rows, u, s, raw, dy, kept, vf, vo, sf, so, off, dec, skip, u, s)
 
 
-KINDS = {"O": "AAA", "G": "AAA", "X": "AAA"}
+KINDS = {"O": "A3", "G": "A3", "X": "A3"}
 ORDER = (
-    "*mo", "*mg", "G1", "O1", "O2", "G0", "O0", "G2", "G1", "*bwd", "*mx", "G1", "O2", "X2",
-    "*grad", "O2", "*out", "G0+G1", "*state", "*tot", "X2", "X0", "G0", "O0+O2", "*pack", "X2",
-    "X1", "X0+G0", "U", "R", "O2", "U", "O0", "U", "G2+X2", "E", "G1", "U", "F", "O1+O0", "E",
-    "G2", "X2", "P", "G0", "F", "O1", "E", "X1+G2", "P", "F", "O0", "R", "P", "E", "O1", "X1",
-    "E", "G2", "R", "F", "X0", "O1", "X1", "F", "O0", "O2", "G0", "G1", "G2", "X2", "X0", "X1",
-    "P", "E", "O1", "F", "K", "X0", "R", "X1", "K", "K", "X0",
+    "*so", "O", "*ko", "*sg", "*bwd", "*state", "G", "U", "O2", "U", "O1", "U", "*grad", "U",
+    "O0", "O2", "*sx", "X", "O1", "*kg", "G2", "*kx", "O0", "G1+O2", "*tot", "G2", "G0+O1",
+    "O2", "*pack", "X1+O0", "E", "G0", "O1", "X0+G2", "R", "O0", "G1", "E", "X2+G0", "X1",
+    "G2", "R", "*out", "E", "G1", "G0", "P", "R", "X2", "E", "G1", "X1", "X0", "P", "O2", "E",
+    "X2", "X1", "E", "K", "P", "X0", "X2", "O0", "O1", "X1", "G2", "G0", "X0", "K", "G1", "X2",
+    "R", "K", "P", "X0",
 )
 
 
@@ -568,28 +643,35 @@
             [jnp.where(which == 0, half, other), jnp.where(which == 0, other, half)]
         )
 
-    def cut(self, array, first, rows, which):
-        return lax.dynamic_slice_in_dim(array, first + which * rows, rows, 0)
-
-    def line_sum(self, array, first, rows):
+    def opening(self, route, value):
+        yield "sent", (yield route, self.hold(value))
+
+    def line_sum(self, own, other, rows):
+        own, other = self.hold((own, other))
+        half = own[rows] + other[rows]
+        half = half + (yield "near", half)
+        half = half + (yield "middle", half)
+        half = jnp.where(self.end, (yield "near", half), half)
+        yield "done", (half, (yield "pair", half))
+
+    def fold_sum(self, own, other, rows):
+        own, other = self.hold((own, other))
+        place = lax.axis_index("dp") >> 2
+        half = own[rows] + other[rows]
+        part = self.take(half, place)
+        part = part + (yield "cross", self.take(half, 1 - place))
+        part = part + (yield "pair", part)
+        half = self.join(part, (yield "cross", part), place)
+        yield "done", (half, (yield "near", half))
+
+    def whole_sum(self, array):
         array = self.hold(array)
-        half = self.cut(array, first, rows // 2, self.side)
-        half = half + (yield "pair", self.cut(array, first, rows // 2, 1 - self.side))
+        half = self.take(array, self.side)
+        half = half + (yield "pair", self.take(array, 1 - self.side))
         half = half + (yield "near", half)
         half = half + (yield "middle", half)
         half = jnp.where(self.end, (yield "near", half), half)
         yield "done", self.join(half, (yield "pair", half), self.side)
-
-    def fold_sum(self, array, first, rows):
-        array = self.hold(array)
-        place = lax.axis_index("dp") >> 2
-        half = self.cut(array, first, rows // 2, self.fold)
-        half = half + (yield "near", self.cut(array, first, rows // 2, 1 - self.fold))
-        part = self.take(half, place)
-        part = part + (yield "cross", self.take(half, 1 - place))
-        part = part + (yield "pair", part)
-        half = self.join(part, (yield "cross", part), place)
-        yield "done", self.join(half, (yield "near", half), self.fold)
 
     def scatter(self, array, axis):
         array = self.hold(array)
@@ -644,79 +726,105 @@
     cols = width // groups
     start = rank * cols
     cuts = width // channels
-
-    wide = tokens.astype(F32)
-    scale = lax.rsqrt(jnp.mean(wide * wide, axis=1, keepdims=True) + EPS)
-    normed = (wide * scale * norm_gain[None, :]).astype(BF16)
+    folds = channels // wide_states
+
     live = (segment >= 0).astype(F32)[:, None]
-    masked = cotangent * live.astype(BF16)
-    gate = nn(normed, gate_weight)
-    values = nn(normed, value_weight)
-    states = nn(normed, state_weight)
-    raw = nn(normed, step_weight)
-    branch_grad = nt(masked, output_weight)
-
     aux, seg_rows, ends = side_columns(segment)
+    normed, gate, values, states, raw, masked, branch_grad = front(
+        aux,
+        tokens,
+        cotangent,
+        norm_gain,
+        gate_weight,
+        value_weight,
+        state_weight,
+        step_weight.T,
+        output_weight,
+    )
     shared = (
         value_filter,
-        value_offset[None, :],
+        value_offset,
         state_filter,
-        state_offset[None, :],
-        step_offset[None, :],
-        decay_log[None, :],
-        skip_gain[None, :],
+        state_offset,
+        step_offset,
+        decay_log,
+        skip_gain,
     )
     scanned, sums, kept = scan_forward(
-        ends, aux, seg_rows, values, states, raw, gate, branch_grad, *shared, inner_gain[None, :]
+        ends, aux, seg_rows, values, states, raw, gate, branch_grad, *shared, inner_gain
     )
     sums = lax.psum(sums, "tensor") / inner_all
     inner_scale = lax.rsqrt(sums[0] + EPS)
     pull = (inner_scale**3 * sums[1])[:, None]
     inner_scale = inner_scale[:, None]
 
-    gate_sig = jax.nn.sigmoid(gate)
-    silu_gate = gate * gate_sig
-    gated = scanned * silu_gate
-    unit_inner = gated * inner_scale
-    branch = (unit_inner * inner_gain[None, :]).astype(BF16)
-    gated_grad = inner_scale * (branch_grad * inner_gain[None, :]) - gated * pull
-    gate_low = (gated_grad * scanned * (gate_sig + silu_gate * (1.0 - gate_sig))).astype(BF16)
-    scanned_grad = gated_grad * silu_gate
-    inner_gain_grad = jnp.sum(branch_grad * unit_inner, axis=0)
+    branch = scanned * (gate * sigmoid(gate)) * inner_scale * inner_gain[None, :]
+    branch = branch.astype(BF16)
+
+    def scale_of(rows):
+        wide = rows.astype(F32)
+        return lax.rsqrt(jnp.mean(wide * wide, axis=1, keepdims=True) + EPS)
+
     env = {}
 
-    def mo(hold):
-        env["O"] = tn(branch, masked)
-        return env["O"]
-
-    def mg(hold):
-        env["G"] = tn(normed, hold(gate_low))
-        return env["G"]
+    def half_of(array, which):
+        return lax.dynamic_slice_in_dim(array, which * (width // 2), width // 2, 1)
+
+    def cut(key, product):
+        def send(hold):
+            env[key] = product(hold, 1 - bit[key])
+            return env[key]
+
+        def keep(hold):
+            env[key + "k"] = product(hold, bit[key])
+            return env[key + "k"]
+
+        return send, keep
+
+    def to_gate(hold):
+        y, gate_in, bg = hold((scanned, gate, branch_grad))
+        gate_sig = sigmoid(gate_in)
+        silu_gate = gate_in * gate_sig
+        gated = y * silu_gate
+        gated_grad = inner_scale * (bg * inner_gain[None, :]) - gated * pull
+        gate_low = gated_grad * y * (gate_sig + silu_gate * (1.0 - gate_sig))
+        env["gate_low"] = gate_low.astype(BF16)
+        env["scanned_grad"] = gated_grad * silu_gate
+        env["inner_gain"] = jnp.sum(bg * gated * inner_scale, axis=0)
+
+    def out_product(hold, which):
+        return tn(branch, half_of(hold(masked), which))
+
+    def gate_product(hold, which):
+        if "gate_low" not in env:
+            to_gate(hold)
+        return tn(half_of(normed, which), hold(env["gate_low"]))
+
+    def value_product(hold, which):
+        return tn(half_of(normed, which), hold(env["low"][0]))
 
     def bwd(hold):
         results = scan_backward(
-            ends, aux, seg_rows, values, states, raw, hold(scanned_grad), kept, *shared
+            ends, aux, seg_rows, values, states, raw, hold(env["scanned_grad"]), kept, *shared
         )
         values_low, upper, lower, steps_low, by_channel, by_state, by_head = results
         env["low"] = (values_low, steps_low, upper, lower)
         env["sums"] = (by_channel, by_state, by_head)
         return values_low
 
-    def mx(hold):
-        env["X"] = tn(normed, hold(env["low"][0]))
-        return env["X"]
-
     def grad(hold):
         values_low, steps_low, upper, lower = hold(env["low"])
         normed_grad = (
-            nt(gate_low, gate_weight)
+            nt(env["gate_low"], gate_weight)
             + nt(steps_low, step_weight)
             + nt(upper, state_weight)
             + nt(lower, state_weight)
             + nt(values_low, value_weight)
         )
         env["R"] = normed_grad
-        unit = hold(tokens).astype(F32) * scale
+        rows = hold(tokens)
+        env["scale"] = scale_of(rows)
+        unit = rows.astype(F32) * env["scale"]
         env["along"] = jnp.sum(normed_grad * unit * norm_gain[None, :], axis=1)
         env["gain"] = jnp.sum(normed_grad * unit, axis=0)
         return normed_grad, env["along"], env["gain"]
@@ -742,12 +850,15 @@
             laid.append(jnp.pad(item, ((0, -item.shape[0] % 8), (0, channels - item.shape[1]))))
         return laid
 
-    def pack(hold):
+    def pack(hold, part):
         by_channel, _, by_head = env["sums"]
         skip_part = jnp.sum(by_channel[5].reshape(heads, -1), axis=1)
+        size = part.shape[0] // folds
+        blocks = [part[i * size :][:size] for i in range(folds)]
         small = rows_of(
+            jnp.concatenate(blocks, axis=1),
             by_channel,
-            inner_gain_grad[None, :],
+            env["inner_gain"][None, :],
             hold(env["maps"]),
             jnp.stack([by_head[0], by_head[1], skip_part]),
         )
@@ -759,31 +870,55 @@
         env["E"] = jnp.concatenate(small + [jnp.zeros((room, channels), F32)])
         return env["E"]
 
+    def unfold(total):
+        blocks = total[: env["heights"][0]]
+        return jnp.concatenate(
+            [blocks[:, i * wide_states :][:, :wide_states] for i in range(folds)]
+        )
+
     def mixed_of(summed):
         token_share = lax.dynamic_slice_in_dim(tokens, start, cols, 1).astype(F32)
         return (token_share + live * summed).astype(BF16)
 
     def tokens_of(share_grad):
-        unit_share = lax.dynamic_slice_in_dim(tokens, start, cols, 1).astype(F32) * scale
+        unit_share = lax.dynamic_slice_in_dim(tokens, start, cols, 1).astype(F32) * env["scale"]
         gain_share = lax.dynamic_slice_in_dim(norm_gain, start, cols, 0)
         cotangent_share = lax.dynamic_slice_in_dim(cotangent, start, cols, 1).astype(F32)
-        return cotangent_share + scale * (
+        return cotangent_share + env["scale"] * (
             share_grad * gain_share[None, :] - unit_share * (env["along"] / width)[:, None]
         )
 
-    tasks = dict(mo=mo, mg=mg, bwd=bwd, mx=mx, grad=grad, state=state, out=out, tot=tot, pack=pack)
     if lax.axis_size("dp") != 8 or groups != 4:
-        for task in tasks.values():
-            task(lambda value: value)
+        def hold(value):
+            return value
+
+        to_gate(hold)
+        for task in (bwd, grad, state, out, tot):
+            task(hold)
+        part = lax.psum_scatter(env["U"], "tensor", scatter_dimension=0, tiled=True)
+        pack(hold, part)
         mixed = mixed_of(lax.psum_scatter(env["P"], "tensor", scatter_dimension=1, tiled=True))
         shared_grad = lax.psum_scatter(env["R"], "tensor", scatter_dimension=1, tiled=True)
         tokens_grad = tokens_of(shared_grad)
-        part = lax.psum_scatter(env["U"], "tensor", scatter_dimension=0, tiled=True)
-        totals = lax.psum((env["O"], env["G"], env["X"], part, env["E"]), "dp")
-        output_grad, gate_weight_grad, value_weight_grad, part, small = totals
-        state_weight_grad = lax.all_gather(part, "tensor", axis=0, tiled=True)
+        output_grad, gate_weight_grad, value_weight_grad, small = lax.psum(
+            (
+                tn(branch, masked),
+                tn(normed, env["gate_low"]),
+                tn(normed, env["low"][0]),
+                env["E"],
+            ),
+            "dp",
+        )
+        state_weight_grad = lax.all_gather(unfold(small), "tensor", axis=0, tiled=True)
     else:
         plan = Schedule()
+        bit = {key: plan.side if KINDS[key][0] == "A" else plan.fold for key in "OGX"}
+        so, ko = cut("O", out_product)
+        sg, kg = cut("G", gate_product)
+        sx, kx = cut("X", value_product)
+        tasks = dict(so=so, ko=ko, sg=sg, kg=kg, sx=sx, kx=kx, bwd=bwd)
+        tasks.update(grad=grad, state=state, out=out, tot=tot)
+        tasks["pack"] = lambda hold: pack(hold, plan.done["U"])
         for entry in ORDER:
             if entry[0] == "*":
                 result = tasks[entry[1:]](plan.hold)
@@ -797,34 +932,42 @@
                     flow = plan.scatter(env[name], 1)
                 elif name == "U":
                     flow = plan.scatter(env[name], 0)
-                elif name == "F":
-                    flow = plan.line_sum(plan.done["U"], 0, plan.done["U"].shape[0])
                 elif name == "K":
-                    flow = plan.gather(plan.done["F"])
+                    flow = plan.gather(unfold(plan.done["E"]))
                 elif name == "E":
-                    flow = plan.line_sum(env["E"], 0, env["E"].shape[0])
+                    flow = plan.whole_sum(env["E"])
+                elif len(name) == 1:
+                    flow = plan.opening("pair" if KINDS[name][0] == "A" else "near", env[name])
                 else:
-                    kinds, array = KINDS[name[0]], env[name[0]]
-                    rows, i = array.shape[0] // len(kinds), int(name[1])
-                    flow = plan.line_sum if kinds[i] == "A" else plan.fold_sum
-                    flow = flow(array, i * rows, rows)
+                    key, i = name[0], int(name[1:])
+                    rows = env[key].shape[0] // int(KINDS[key][1:])
+                    flow = plan.line_sum if KINDS[key][0] == "A" else plan.fold_sum
+                    part = slice(i * rows, (i + 1) * rows)
+                    flow = flow(env[key + "k"], plan.flows[key][1], part)
                 plan.add(name, flow)
             plan.step(names)
         mixed = mixed_of(plan.done["P"])
         tokens_grad = tokens_of(plan.done["R"])
         state_weight_grad = plan.done["K"]
-        output_grad, gate_weight_grad, value_weight_grad = (
-            jnp.concatenate([plan.done[f"{key}{i}"] for i in range(len(KINDS[key]))])
-            for key in "OGX"
-        )
+        totals = {}
+        for key in "OGX":
+            got = [plan.done[f"{key}{i}"] for i in range(int(KINDS[key][1:]))]
+            low = [jnp.where(bit[key] == 0, half, other) for half, other in got]
+            high = [jnp.where(bit[key] == 0, other, half) for half, other in got]
+            if key == "O":
+                sides = [jnp.concatenate([lo, hi], axis=1) for lo, hi in zip(low, high)]
+                totals[key] = jnp.concatenate(sides)
+            else:
+                totals[key] = jnp.concatenate(low + high)
+        output_grad, gate_weight_grad, value_weight_grad = (totals[key] for key in "OGX")
         small = plan.done["E"]
     parts = []
     for height in env["heights"]:
         parts.append(small[:height])
         small = small[height:]
-    chan, inner_grad, state_pair, head = parts[:4]
-    gain_grad = jnp.concatenate([part[0] for part in parts[4 : 4 + cuts]])
-    step_grad = jnp.concatenate([part[:heads] for part in parts[4 + cuts :]], axis=1)
+    chan, inner_grad, state_pair, head = parts[1:5]
+    gain_grad = jnp.concatenate([part[0] for part in parts[5 : 5 + cuts]])
+    step_grad = jnp.concatenate([part[:heads] for part in parts[5 + cuts :]], axis=1)
     state_pair = state_pair[:, :wide_states]
     off, dec, skip = (head[i, :heads] for i in range(3))
     return (

time: 482 us -> 436 us (0.905)
  waiting for transfers between devices: 181 us -> 149 us
  starting transfers between devices: 75.6 us -> 55.2 us
  other arithmetic: 53.8 us -> 73 us
  Pallas kernels: 41.7 us -> 57.9 us
  matrix products: 64.7 us -> 49.7 us
  local copies, waits for them, and re-layouts: 33.7 us -> 22.3 us
    ppermute x60 -> x50, waiting for transfers between devices: 181 us -> 149 us  [step(): got = lax.ppermute(value, ('dp', 'tensor'), self.route[route])]
    ppermute x60 -> x50, starting transfers between devices: 75.6 us -> 55.2 us  [step(): got = lax.ppermute(value, ('dp', 'tensor'), self.route[route])]
    pallas_call x0 -> x1, Pallas kernels: none -> 16.3 us  [front(): pl.pallas_call(front_kernel, name='front', grid=(length // rows,), in_spe...]
    dynamic_slice x11 -> x1, local copies, waits for them, and re-layouts: 16.1 us -> 0.03 us  [take(): return lax.dynamic_slice_in_dim(piece, which * rows, rows, 0)]
    dot_general x5 -> x1, matrix products: 18.3 us -> 2.6 us  [nn(): lax.dot_general(a, b, (((1,), (0,)), ((), ())), precision=precision, pref...]
    convert_element_type x1 -> x2, other arithmetic: 2.82 us -> 9.96 us  [the longest x1 6.19 us: to_gate(): env['gate_low'] = gate_low.astype(BF16)]
    dot_general x6 -> x9, matrix products: 17.7 us -> 24.4 us  [tn(): lax.dot_general(a, b, (((0,), (0,)), ((), ())), precision=precision, pref...]
    mul x1 -> x0, other arithmetic: 6.37 us -> none  [on_device(): scanned_grad = gated_grad * silu_gate]
  transfers between devices with their start and end apart: 60 -> 50, of which waited for: 23 -> 19; matrix products, arithmetic and copies ran while one was open for 22% -> 29% of each run, Pallas kernels for 6% -> 7%
where the time goes in v1:
time: 436 us; the launch traced here: 429 us
  waiting for transfers between devices  149 us (34%)
  other arithmetic  73 us (17%)
  Pallas kernels  57.9 us (13%)
  starting transfers between devices  55.2 us (13%)
  matrix products  49.7 us (11%)
  local copies, waits for them, and re-layouts  22.3 us (5%)
  blocking collectives  19.9 us (5%)
    ppermute x50, waiting for transfers between devices, step(): got = lax.ppermute(value, ('dp', 'tensor'), self.route[route])  149 us
    ppermute x50, starting transfers between devices, step(): got = lax.ppermute(value, ('dp', 'tensor'), self.route[route])  55.2 us
    pallas_call x1, Pallas kernels, scan_backward(): pl.pallas_call(backward_kernel, name='scan_backward', cost_estimate=pl.Co...  28.6 us
    dot_general x9, matrix products, tn(): lax.dot_general(a, b, (((0,), (0,)), ((), ())), precision=precision, pref...  24.4 us
    dot_general x5, matrix products, nt(): lax.dot_general(a, b, (((1,), (1,)), ((), ())), precision=precision, pref...  22.8 us
    pallas_call x1, Pallas kernels, front(): pl.pallas_call(front_kernel, name='front', grid=(length // rows,), in_spe...  16.3 us
    pallas_call x1, Pallas kernels, scan_forward(): pl.pallas_call(forward_kernel, name='scan_forward', cost_estimate=pl.Cost...  13.1 us
    add x9, other arithmetic, line_sum(): half = half + (yield ('near', half))  13 us
  transfers between devices with their start and end apart: 50, of which 19 were waited for; matrix products, arithmetic and copies ran while one was open for 29% of the time, Pallas kernels for 7%

profile of v1, /device:TPU:0, one launch (start us, length us, event | category | flops | bytes accessed | tf_op | source)
XLA Modules:
  0.0 428.9 jit_solution(13399186461751983791)
XLA Ops:
  4.7 16.3 %front.1 = (bf16[1024,1536]{1,0:T(8,128)(2,1)}, f32[1024,768]{1,0:T(8,128)}, f32[1024,768]{1,0:T(8,128)}, f32[1024,256]{1,0:T(8,128)}, f32[1024,12]{1,0:T(8,128)...) custom-call(f32[1024,8]{1,0:T(8,128)} %copy.41.live_ref.aux_ref, bf16[1024,1536]{1,0:T(8,128)(2,1)} %tokens_ref.1, ...), custom_call_target="tpu_custom_call" | custom-call | tf_op jit(solution)/shard_map/front/pallas_call | solution.py:153
  21.0 13.1 %scan_forward.1 = (f32[1024,768]{1,0:T(8,128)}, f32[2,1024]{1,0:T(2,128)}, bf16[8,128,768]{2,1,0:T(8,128)(2,1)}) custom-call(f32[9]{0:T(128)} %pad_maximum_fusion.3.ends, f32[1024,8]{1,0:T(8,128)} %copy.41.live_ref.aux_ref, f32[8,128]{1,0:T(8,128)} %copy-done.42, f32[1024,768]{1,0:T(8,128)} %get-tuple-element.111.u_ref.ubef_ref, ...), custom_call_target="tpu_custom_call" | custom-call | flops 3221225472 | bytes 14680064 | tf_op jit(solution)/shard_map/scan_forward/pallas_call | solution.py:459
  34.1 8.6 %psum.28 = f32[2,1024]{1,0:T(2,128)S(1)} all-reduce(f32[2,1024]{1,0:T(2,128)} %get-tuple-element.117), channel_id=1, replica_groups=mesh['dp'=8,'tensor'=4] {'tensor'}, use_global_device_ids=true, to_apply=%region_0.1 | all-reduce | flops 2048 | bytes 16384 | tf_op jit(solution)/shard_map/psum | solution.py:756
  46.6 4.9 %fusion.13 = f32[768,768]{1,0:T(8,128)} fusion(bf16[1024,768]{1,0:T(8,128)(2,1)S(1)} %multiply_convert_fusion.1, bf16[1024,1536]{1,0:T(8,128)(2,1)} %get-tuple-element.119, s32[]{:T(128)S(6)} %select_n.197), kind=kOutput, calls=%fused_computation.28 | convolution fusion | flops 1207959552 | bytes 5505028 | tf_op jit(solution)/shard_map/dot_general | solution.py:31
  57.4 6.2 %multiply_convert_fusion = (bf16[1024,768]{1,0:T(8,128)(2,1)S(1)}, f32[1024,768]{1,0:T(8,128)}, f32[768]{0:T(1024)S(1)}) fusion(f32[1024,768]{1,0:T(8,128)} %get-tuple-element.121, f32[1024,768]{1,0:T(8,128)S(1)} %copy-done.3, f32[1024]{0:T(1024)S(1)} %fusion.37, f32[1024,768]{1,0:T(8,128)} %get-tuple-element.120.bg_ref, f32[768]{0:T(1024)S(1)} %copy-done.43, ...), kind=kLoop, calls=%fused_computation.9 | loop fusion | flops 14941440 | bytes 14170112 | tf_op jit(solution)/shard_map/convert_element_type | solution.py:791
  66.5 28.6 %scan_backward.1 = (bf16[1024,768]{1,0:T(8,128)(2,1)}, bf16[1024,256]{1,0:T(8,128)(2,1)}, bf16[1024,256]{1,0:T(8,128)(2,1)}, bf16[1024,12]{1,0:T(8,128)(2,1)}, f...) custom-call(f32[9]{0:T(128)} %pad_maximum_fusion.3.ends, f32[1024,8]{1,0:T(8,128)} %copy.41.live_ref.aux_ref, ...), custom_call_target="tpu_custom_call" | custom-call | flops 8053063680 | bytes 16777216 | tf_op jit(solution)/shard_map/scan_backward/pallas_call | solution.py:516
  105.7 6.1 %fusion.57 = f32[1024,1536]{1,0:T(8,128)} fusion(bf16[1024,768]{1,0:T(8,128)(2,1)} %copy-done.26, bf16[1536,768]{1,0:T(8,128)(2,1)S(1)} %copy-done.14), kind=kOutput, calls=%fused_computation.174 | convolution fusion | flops 2415919104 | bytes 10223616 | tf_op jit(solution)/shard_map/dot_general | solution.py:25
  120.8 6.1 %fusion.61 = f32[1024,1536]{1,0:T(8,128)} fusion(bf16[1024,768]{1,0:T(8,128)(2,1)} %get-tuple-element.151, bf16[1536,768]{1,0:T(8,128)(2,1)S(1)} %copy-done.15), kind=kOutput, calls=%fused_computation.178 | convolution fusion | flops 2415919104 | bytes 10223616 | tf_op jit(solution)/shard_map/dot_general | solution.py:25
  131.7 8.6 %fusion.2 = (f32[1536]{0:T(1024)}, f32[1024]{0:T(1024)}, f32[1024,1536]{1,0:T(8,128)}) fusion(bf16[1024,1536]{1,0:T(8,128)(2,1)S(1)} %copy-done, f32[1024]{0:T(1024)S(1)} %add_rsqrt_fusion, f32[1536]{0:T(1024)S(1)} %copy-done.37, f32[1024,1536]{1,0:T(8,128)} %fusion.61, bf16[1024,256]{1,0:T(8,128)(2,1)S(1)} %copy-done.32, ...), kind=kOutput, calls=%fused_computation.7 | convolution fusion | flops 821032448 | bytes 35934208 | tf_op jit(solution)/shard_map/dot_general | solution.py:25
  177.6 11.3 %all-reduce.13 = (f32[1024]{0:T(1024)S(1)}, f32[1536]{0:T(1024)S(1)}, f32[8,256]{1,0:T(8,128)S(1)}) all-reduce(f32[1024]{0:T(1024)S(1)} %copy-done.40, f32[1536]{0:T(1024)S(1)} %copy-done.38, f32[8,256]{1,0:T(8,128)S(1)} %copy-done.46), channel_id=1, replica_groups=mesh['dp'=8,'tensor'=4] {'tensor'}, use_global_device_ids=true, to_apply=%region_4.5 | all-reduce | flops 4608 | bytes 36864 | tf_op jit(solution)/shard_map/psum | solution.py:842
  194.8 10.0 %collective-permute-done.13 = f32[256,768]{1,0:T(8,128)} collective-permute-done((f32[256,768]{1,0:T(8,128)}, f32[256,768]{1,0:T(8,128)}, u32[]{:S(2)}, u32[]{:S(2)}) %collective-permute-start.13) | collective-permute-done | bytes 786464 | tf_op jit(solution)/shard_map/ppermute | solution.py:632
  207.8 10.7 %collective-permute-done.5 = f32[768,768]{1,0:T(8,128)} collective-permute-done((f32[768,768]{1,0:T(8,128)}, f32[768,768]{1,0:T(8,128)}, u32[]{:S(2)}, u32[]{:S(2)}) %collective-permute-start.5) | collective-permute-done | bytes 2359328 | tf_op jit(solution)/shard_map/ppermute | solution.py:632
  227.7 13.2 %collective-permute-done.17 = f32[256,768]{1,0:T(8,128)S(1)} collective-permute-done((f32[256,768]{1,0:T(8,128)S(1)}, f32[256,768]{1,0:T(8,128)S(1)}, u32[]{:S(2)}, u32[]{:S(2)}) %collective-permute-start.17) | collective-permute-done | bytes 786464 | tf_op jit(solution)/shard_map/ppermute | solution.py:632
  248.6 9.1 %collective-permute-done.25 = f32[256,768]{1,0:T(8,128)S(1)} collective-permute-done((f32[256,768]{1,0:T(8,128)S(1)}, f32[256,768]{1,0:T(8,128)S(1)}, u32[]{:S(2)}, u32[]{:S(2)}) %collective-permute-start.25) | collective-permute-done | bytes 786464 | tf_op jit(solution)/shard_map/ppermute | solution.py:632
  257.8 4.8 %collective-permute-done.48 = f32[256,768]{1,0:T(8,128)S(1)} collective-permute-done((f32[256,768]{1,0:T(8,128)S(1)}, f32[256,768]{1,0:T(8,128)S(1)}, u32[]{:S(2)}, u32[]{:S(2)}) %collective-permute-start.48) | collective-permute-done | bytes 786464 | tf_op jit(solution)/shard_map/ppermute | solution.py:632
  267.5 10.5 %collective-permute-done.21 = f32[104,768]{1,0:T(8,128)S(1)} collective-permute-done((f32[104,768]{1,0:T(8,128)S(1)}, f32[104,768]{1,0:T(8,128)S(1)}, u32[]{:S(2)}, u32[]{:S(2)}) %collective-permute-start.21) | collective-permute-done | bytes 319520 | tf_op jit(solution)/shard_map/ppermute | solution.py:632
  284.4 12.9 %collective-permute-start.26 = (f32[104,768]{1,0:T(8,128)S(1)}, f32[104,768]{1,0:T(8,128)S(1)}, u32[]{:S(2)}, u32[]{:S(2)}) collective-permute-start(f32[104,768]{1,0:T(8,128)S(1)} %add.299), channel_id=1, source_target_pairs={{0,8},{1,9},{2,10},{3,11},{4,12},{5,13},{6,14},{7,15},{8,0},{9,1},... | collective-permute-start | bytes 958472 | tf_op jit(solution)/shard_map/ppermute | solution.py:632
  300.3 6.3 %collective-permute-done.26 = f32[104,768]{1,0:T(8,128)S(1)} collective-permute-done((f32[104,768]{1,0:T(8,128)S(1)}, f32[104,768]{1,0:T(8,128)S(1)}, u32[]{:S(2)}, u32[]{:S(2)}) %collective-permute-start.26) | collective-permute-done | bytes 319520 | tf_op jit(solution)/shard_map/ppermute | solution.py:632
  310.1 17.0 %collective-permute-done.36 = f32[256,768]{1,0:T(8,128)S(1)} collective-permute-done((f32[256,768]{1,0:T(8,128)S(1)}, f32[256,768]{1,0:T(8,128)S(1)}, u32[]{:S(2)}, u32[]{:S(2)}) %collective-permute-start.36) | collective-permute-done | bytes 786464 | tf_op jit(solution)/shard_map/ppermute | solution.py:632
  338.2 9.3 %collective-permute-done.30 = f32[256,768]{1,0:T(8,128)S(1)} collective-permute-done((f32[256,768]{1,0:T(8,128)S(1)}, f32[256,768]{1,0:T(8,128)S(1)}, u32[]{:S(2)}, u32[]{:S(2)}) %collective-permute-start.30) | collective-permute-done | bytes 786464 | tf_op jit(solution)/shard_map/ppermute | solution.py:632
  348.7 13.8 %collective-permute-done.44 = f32[256,768]{1,0:T(8,128)S(1)} collective-permute-done((f32[256,768]{1,0:T(8,128)S(1)}, f32[256,768]{1,0:T(8,128)S(1)}, u32[]{:S(2)}, u32[]{:S(2)}) %collective-permute-start.44) | collective-permute-done | bytes 786464 | tf_op jit(solution)/shard_map/ppermute | solution.py:632
  382.2 11.3 %collective-permute-done.38 = f32[384,256]{1,0:T(8,128)} collective-permute-done((f32[384,256]{1,0:T(8,128)S(1)}, f32[384,256]{1,0:T(8,128)}, u32[]{:S(2)}, u32[]{:S(2)}) %collective-permute-start.38) | collective-permute-done | bytes 393248 | tf_op jit(solution)/shard_map/ppermute | solution.py:632
  401.4 10.1 %collective-permute-done.45 = f32[256,768]{1,0:T(8,128)S(1)} collective-permute-done((f32[256,768]{1,0:T(8,128)S(1)}, f32[256,768]{1,0:T(8,128)S(1)}, u32[]{:S(2)}, u32[]{:S(2)}) %collective-permute-start.45) | collective-permute-done | bytes 786464 | tf_op jit(solution)/shard_map/ppermute | solution.py:632
  416.7 8.6 %collective-permute-done.42 = f32[256,768]{1,0:T(8,128)S(1)} collective-permute-done((f32[256,768]{1,0:T(8,128)S(1)}, f32[256,768]{1,0:T(8,128)S(1)}, u32[]{:S(2)}, u32[]{:S(2)}) %collective-permute-start.42) | collective-permute-done | bytes 786464 | tf_op jit(solution)/shard_map/ppermute | solution.py:632
  (311 shorter events, 169.7 us)
Async XLA Ops:
  51.4 63.7 %collective-permute-start.1 = (f32[768,768]{1,0:T(8,128)}, f32[768,768]{1,0:T(8,128)}, u32[]{:S(2)}, u32[]{:S(2)}) collective-permute-start(f32[768,768]{1,0:T(8,128)} %fusion.13), channel_id=1, source_target_pairs={{0,4},{1,5},{2,6},{3,7},{4,0},{5,1},{6,2},{7,3},{8,12},{9,13},{10,... | collective-permute-start | bytes 7077896 | tf_op jit(solution)/shard_map/ppermute | solution.py:632
  99.6 58.5 %collective-permute-start.4 = (f32[768,768]{1,0:T(8,128)}, f32[768,768]{1,0:T(8,128)}, u32[]{:S(2)}, u32[]{:S(2)}) collective-permute-start(f32[768,768]{1,0:T(8,128)} %fusion.21), channel_id=1, source_target_pairs={{0,4},{1,5},{2,6},{3,7},{4,0},{5,1},{6,2},{7,3},{8,12},{9,13},{10,... | collective-permute-start | bytes 7077896 | tf_op jit(solution)/shard_map/ppermute | solution.py:632
  102.1 39.6 %collective-permute-start.11 = (f32[384,256]{1,0:T(8,128)}, f32[384,256]{1,0:T(8,128)}, u32[]{:S(2)}, u32[]{:S(2)}) collective-permute-start(f32[384,256]{1,0:T(8,128)} %get-tuple-element.240), channel_id=1, source_target_pairs={{0,1},{1,0},{2,3},{3,2},{4,5},{5,4},{6,7},{7,6},{8,9},{9,8},{10,11... | collective-permute-start | bytes 1179656 | tf_op jit(solution)/shard_map/ppermute | solution.py:632
  141.7 29.2 %collective-permute-start.7 = (f32[256,768]{1,0:T(8,128)S(1)}, f32[256,768]{1,0:T(8,128)S(1)}, u32[]{:S(2)}, u32[]{:S(2)}) collective-permute-start(f32[256,768]{1,0:T(8,128)S(1)} %slice_add_fusion.6), channel_id=1, source_target_pairs={{0,8},{1,9},{2,10},{3,11},{4,12},{5,13},{6,14},{7,15},{8,0},{9,1},... | collective-permute-start | bytes 2359304 | tf_op jit(solution)/shard_map/ppermute | solution.py:632
  156.6 34.0 %collective-permute-start.9 = (f32[256,768]{1,0:T(8,128)}, f32[256,768]{1,0:T(8,128)}, u32[]{:S(2)}, u32[]{:S(2)}) collective-permute-start(f32[256,768]{1,0:T(8,128)} %add.271), channel_id=1, source_target_pairs={{0,1},{1,0},{2,3},{3,2},{4,5},{5,4},{6,7},{7,6},{8,16},{9,17},{10,... | collective-permute-start | bytes 2359304 | tf_op jit(solution)/shard_map/ppermute | solution.py:632
  164.0 54.5 %collective-permute-start.5 = (f32[768,768]{1,0:T(8,128)}, f32[768,768]{1,0:T(8,128)}, u32[]{:S(2)}, u32[]{:S(2)}) collective-permute-start(f32[768,768]{1,0:T(8,128)} %fusion.19), channel_id=1, source_target_pairs={{0,4},{1,5},{2,6},{3,7},{4,0},{5,1},{6,2},{7,3},{8,12},{9,13},{10,... | collective-permute-start | bytes 7077896 | tf_op jit(solution)/shard_map/ppermute | solution.py:632
  172.0 46.5 %collective-permute-start.14 = (f32[256,768]{1,0:T(8,128)}, f32[256,768]{1,0:T(8,128)}, u32[]{:S(2)}, u32[]{:S(2)}) collective-permute-start(f32[256,768]{1,0:T(8,128)} %add.275), channel_id=1, source_target_pairs={{0,1},{1,0},{2,3},{3,2},{4,5},{5,4},{6,7},{7,6},{8,16},{9,17},{10,... | collective-permute-start | bytes 2359304 | tf_op jit(solution)/shard_map/ppermute | solution.py:632
  174.5 30.3 %collective-permute-start.13 = (f32[256,768]{1,0:T(8,128)}, f32[256,768]{1,0:T(8,128)}, u32[]{:S(2)}, u32[]{:S(2)}) collective-permute-start(f32[256,768]{1,0:T(8,128)} %get-tuple-element.223), channel_id=1, source_target_pairs={{0,8},{1,9},{2,10},{3,11},{4,12},{5,13},{6,14},{7,15},{8,0},{9,1},... | collective-permute-start | bytes 2359304 | tf_op jit(solution)/shard_map/ppermute | solution.py:632
  190.5 32.4 %collective-permute-start.15 = (f32[256,768]{1,0:T(8,128)S(1)}, f32[256,768]{1,0:T(8,128)S(1)}, u32[]{:S(2)}, u32[]{:S(2)}) collective-permute-start(f32[256,768]{1,0:T(8,128)S(1)} %add.278), channel_id=1, source_target_pairs={{0,1},{1,0},{2,3},{3,2},{4,5},{5,4},{6,7},{7,6},{8,16},{9,17},{10,... | collective-permute-start | bytes 2359304 | tf_op jit(solution)/shard_map/ppermute | solution.py:632
  206.0 92.7 %collective-permute-start.49 = (f32[256,768]{1,0:T(8,128)S(1)}, f32[256,768]{1,0:T(8,128)S(1)}, u32[]{:S(2)}, u32[]{:S(2)}) collective-permute-start(f32[256,768]{1,0:T(8,128)S(1)} %broadcast_select_fusion.17), channel_id=1, source_target_pairs={{0,4},{1,5},{2,6},{3,7},{4,0},{5,1},{6,2},{7,3},{8,12},{9,13},{10,... | collective-permute-start | bytes 2359304 | tf_op jit(solution)/shard_map/ppermute | solution.py:632
  224.3 33.5 %collective-permute-start.25 = (f32[256,768]{1,0:T(8,128)S(1)}, f32[256,768]{1,0:T(8,128)S(1)}, u32[]{:S(2)}, u32[]{:S(2)}) collective-permute-start(f32[256,768]{1,0:T(8,128)S(1)} %get-tuple-element.217), channel_id=1, source_target_pairs={{0,8},{1,9},{2,10},{3,11},{4,12},{5,13},{6,14},{7,15},{8,0},{9,1},... | collective-permute-start | bytes 2359304 | tf_op jit(solution)/shard_map/ppermute | solution.py:632
  245.6 34.2 %collective-permute-start.19 = (f32[256,768]{1,0:T(8,128)S(1)}, f32[256,768]{1,0:T(8,128)S(1)}, u32[]{:S(2)}, u32[]{:S(2)}) collective-permute-start(f32[256,768]{1,0:T(8,128)S(1)} %get-tuple-element.215), channel_id=1, source_target_pairs={{0,8},{1,9},{2,10},{3,11},{4,12},{5,13},{6,14},{7,15},{8,0},{9,1},... | collective-permute-start | bytes 2359304 | tf_op jit(solution)/shard_map/ppermute | solution.py:632
  262.7 36.0 %collective-permute-start.28 = (f32[256,768]{1,0:T(8,128)S(1)}, f32[256,768]{1,0:T(8,128)S(1)}, u32[]{:S(2)}, u32[]{:S(2)}) collective-permute-start(f32[256,768]{1,0:T(8,128)S(1)} %fusion.28), channel_id=1, source_target_pairs={{0,1},{1,0},{2,3},{3,2},{4,5},{5,4},{6,7},{7,6},{8,16},{9,17},{10,... | collective-permute-start | bytes 2359304 | tf_op jit(solution)/shard_map/ppermute | solution.py:632
  298.7 31.8 %collective-permute-start.34 = (f32[1024,384]{1,0:T(8,128)S(1)}, f32[1024,384]{1,0:T(8,128)S(1)}, u32[]{:S(2)}, u32[]{:S(2)}) collective-permute-start(f32[1024,384]{1,0:T(8,128)S(1)} %get-tuple-element.231), channel_id=1, source_target_pairs={{0,1},{1,0},{2,3},{3,2},{4,5},{5,4},{6,7},{7,6},{8,9},{9,8},{10,11... | collective-permute-start | bytes 4718600 | tf_op jit(solution)/shard_map/ppermute | solution.py:632
  299.6 30.9 %collective-permute-start.32 = (f32[1024,384]{1,0:T(8,128)S(1)}, f32[1024,384]{1,0:T(8,128)S(1)}, u32[]{:S(2)}, u32[]{:S(2)}) collective-permute-start(f32[1024,384]{1,0:T(8,128)S(1)} %get-tuple-element.229), channel_id=1, source_target_pairs={{0,1},{1,0},{2,3},{3,2},{4,5},{5,4},{6,7},{7,6},{8,9},{9,8},{10,11... | collective-permute-start | bytes 4718600 | tf_op jit(solution)/shard_map/ppermute | solution.py:632
  299.7 36.9 %collective-permute-start.35 = (f32[1024,384]{1,0:T(8,128)S(1)}, f32[1024,384]{1,0:T(8,128)S(1)}, u32[]{:S(2)}, u32[]{:S(2)}) collective-permute-start(f32[1024,384]{1,0:T(8,128)S(1)} %get-tuple-element.230), channel_id=1, source_target_pairs={{0,2},{1,3},{2,0},{3,1},{4,6},{5,7},{6,4},{7,5},{8,10},{9,11},{10,... | collective-permute-start | bytes 4718600 | tf_op jit(solution)/shard_map/ppermute | solution.py:632
  308.9 38.7 %collective-permute-start.27 = (f32[104,768]{1,0:T(8,128)S(1)}, f32[104,768]{1,0:T(8,128)S(1)}, u32[]{:S(2)}, u32[]{:S(2)}) collective-permute-start(f32[104,768]{1,0:T(8,128)S(1)} %broadcast_select_fusion.20), channel_id=1, source_target_pairs={{0,4},{1,5},{2,6},{3,7},{4,0},{5,1},{6,2},{7,3},{8,12},{9,13},{10,... | collective-permute-start | bytes 958472 | tf_op jit(solution)/shard_map/ppermute | solution.py:632
  330.6 31.9 %collective-permute-start.44 = (f32[256,768]{1,0:T(8,128)S(1)}, f32[256,768]{1,0:T(8,128)S(1)}, u32[]{:S(2)}, u32[]{:S(2)}) collective-permute-start(f32[256,768]{1,0:T(8,128)S(1)} %add.301), channel_id=1, source_target_pairs={{0,8},{1,9},{2,10},{3,11},{4,12},{5,13},{6,14},{7,15},{8,0},{9,1},... | collective-permute-start | bytes 2359304 | tf_op jit(solution)/shard_map/ppermute | solution.py:632
  347.6 48.6 %collective-permute-start.37 = (f32[256,768]{1,0:T(8,128)S(1)}, f32[256,768]{1,0:T(8,128)S(1)}, u32[]{:S(2)}, u32[]{:S(2)}) collective-permute-start(f32[256,768]{1,0:T(8,128)S(1)} %broadcast_select_fusion.9), channel_id=1, source_target_pairs={{0,4},{1,5},{2,6},{3,7},{4,0},{5,1},{6,2},{7,3},{8,12},{9,13},{10,... | collective-permute-start | bytes 2359304 | tf_op jit(solution)/shard_map/ppermute | solution.py:632
  348.2 64.3 %collective-permute-start.33 = (f32[1024,384]{1,0:T(8,128)}, f32[1024,384]{1,0:T(8,128)}, u32[]{:S(2)}, u32[]{:S(2)}) collective-permute-start(f32[1024,384]{1,0:T(8,128)} %dynamic-slice_add_fusion), channel_id=1, source_target_pairs={{0,2},{1,3},{2,0},{3,1},{4,6},{5,7},{6,4},{7,5},{8,10},{9,11},{10,... | collective-permute-start | bytes 4718600 | tf_op jit(solution)/shard_map/ppermute | solution.py:632
  362.9 30.6 %collective-permute-start.38 = (f32[384,256]{1,0:T(8,128)S(1)}, f32[384,256]{1,0:T(8,128)}, u32[]{:S(2)}, u32[]{:S(2)}) collective-permute-start(f32[384,256]{1,0:T(8,128)S(1)} %fusion.23), channel_id=1, source_target_pairs={{0,2},{1,3},{2,0},{3,1},{4,6},{5,7},{6,4},{7,5},{8,10},{9,11},{10,... | collective-permute-start | bytes 1179656 | tf_op jit(solution)/shard_map/ppermute | solution.py:632
  380.5 31.0 %collective-permute-start.45 = (f32[256,768]{1,0:T(8,128)S(1)}, f32[256,768]{1,0:T(8,128)S(1)}, u32[]{:S(2)}, u32[]{:S(2)}) collective-permute-start(f32[256,768]{1,0:T(8,128)S(1)} %broadcast_select_fusion.6), channel_id=1, source_target_pairs={{0,4},{1,5},{2,6},{3,7},{4,0},{5,1},{6,2},{7,3},{8,12},{9,13},{10,... | collective-permute-start | bytes 2359304 | tf_op jit(solution)/shard_map/ppermute | solution.py:632
  393.5 31.8 %collective-permute-start.42 = (f32[256,768]{1,0:T(8,128)S(1)}, f32[256,768]{1,0:T(8,128)S(1)}, u32[]{:S(2)}, u32[]{:S(2)}) collective-permute-start(f32[256,768]{1,0:T(8,128)S(1)} %broadcast_select_fusion.7), channel_id=1, source_target_pairs={{0,4},{1,5},{2,6},{3,7},{4,0},{5,1},{6,2},{7,3},{8,12},{9,13},{10,... | collective-permute-start | bytes 2359304 | tf_op jit(solution)/shard_map/ppermute | solution.py:632
  396.2 29.8 %collective-permute-start.46 = (f32[768,256]{1,0:T(8,128)S(1)}, f32[768,256]{1,0:T(8,128)S(1)}, u32[]{:S(2)}, u32[]{:S(2)}) collective-permute-start(f32[768,256]{1,0:T(8,128)S(1)} %pad_maximum_fusion), channel_id=1, source_target_pairs={{0,1},{1,0},{2,3},{3,2},{4,5},{5,4},{6,7},{7,6},{8,9},{9,8},{10,11... | collective-permute-start | bytes 2359304 | tf_op jit(solution)/shard_map/ppermute | solution.py:632
  (78 other events, 1020.2 us)
